TPU v7x, 1024 devices: a whole 4x4x32 slice. The times are simulated.
1024 devices in a mesh: cells: 16 (over x, y), wall: 64 (over z, core).
Axes of the slice: x: 4, y: 4, z: 32, core: 2. Of those that a mesh axis runs over, the one named last changes fastest.
Arguments:
- shape_coef: bfloat16 [3, 289, 262144], P(None, None, ('cells', 'wall')), may hold values from -3 to 3
- force_coef: bfloat16 [3, 289, 262144], P(None, None, ('cells', 'wall')), may hold values from -1.5 to 1.5
- near_cell: int32 [65536], P(('cells', 'wall')), may hold values from 0 to 255
- near_dest: int32 [65536], P(('cells', 'wall')), may hold values from 0 to 63, as said below
- near_slot: int32 [65536], P(('cells', 'wall')), may hold values from 0 to 1
- panel_centers: float32 [2048, 384], P(('cells', 'wall')), may hold values from -2 to 2
- near_blocks: bfloat16 [2048, 2, 384, 384], P(('cells', 'wall')), may hold values from -0.15625 to 0.15625
- near_pick: int32 [2048], P(('cells', 'wall')), may hold values from 0 to 1
- src_basis: float32 [2048, 384, 16], P(('cells', 'wall')), may hold values from -0.3125 to 0.3125
- far_couple: float32 [2048, 8, 16, 16], P(('cells', 'wall')), may hold values from -0.5 to 0.5
- far_src: int32 [2048, 8], P(('cells', 'wall')), may hold values from 0 to 2047
- far_rank: int32 [2048, 8], P(('cells', 'wall')), may hold values from 1 to 16
- tgt_basis: float32 [2048, 16, 384], P(('cells', 'wall')), may hold values from -1.5 to 1.5
- cluster_slot: int32 [2048], replicated, may hold values from 0 to 2047, each once
Outputs:
- surface: bfloat16 [3, 578, 262144], P(None, None, ('cells', 'wall'))
- density: float32 [2048, 384], P(('cells', 'wall'))
Inputs may be any that keep to these rules, and one draw needn't show every extreme that they name: `near_cell`: A cell of the row's own device block of 256 cells; each device holds 64 rows. `near_dest`: among the 64 rows of one device no value appears more than 2 times; in each group of 64 devices along the wall axis some value appears exactly 2 times among the rows of every device of the group. `cluster_slot`: each of 0 to 2047 appears once.
All inputs are finite; a program needn't handle non-finite values.
Results may differ from a plain program's by a relative error of at most 0.0062.
Values may be sent and summed in bfloat16 or wider, within the bound.
No kernel may reach another device: no remote copies, remote signals or barrier semaphores. Data moves between devices by JAX's collectives and lax.ppermute only.
A program may use at most 32 MiB of HBM per device.

v0:
```python
import math

import jax
import jax.numpy as jnp
import numpy as np
from jax import lax
from jax.sharding import Mesh
from jax.sharding import PartitionSpec as P

ORDER = 16
ITERS = 2
WALL = ("wall_0", "wall_1")
CELLS_WALL = ("cells_0", "cells_1", "wall_0", "wall_1")


soft_core = 0.25
stokes_scale = 1.0 / (8.0 * math.pi)


def shifted(array, axis, by):
    devices = lax.axis_size(axis)
    return lax.ppermute(array, axis, [(i, (i + by) % devices) for i in range(devices)])


def laid_out(pieces, dim):
    pieces = jnp.moveaxis(pieces, 0, dim)
    shape = pieces.shape
    return pieces.reshape(*shape[:dim], shape[dim] * shape[dim + 1], *shape[dim + 2 :])


def gather_in_order(array, axes, order):
    pieces = array
    for k in order:
        pieces = lax.all_gather(pieces, axes[k])
    done = order[::-1]
    back = [done.index(k) for k in range(len(axes))]
    pieces = pieces.transpose(*back, *range(len(axes), pieces.ndim))
    return pieces.reshape(-1, *array.shape)


def whole_of(array, axes, order, dim):
    return laid_out(gather_in_order(array, axes, order), dim)


def harmonics(order):
    lat_count = order + 1
    polar_angle = np.pi * (np.arange(lat_count) + 0.5) / lat_count
    azimuth = np.pi * np.arange(2 * lat_count) / lat_count
    cos_polar = np.repeat(np.cos(polar_angle), 2 * lat_count)
    sin_polar = np.repeat(np.sin(polar_angle), 2 * lat_count)
    az_grid = np.tile(azimuth, lat_count)
    legendre = {}
    legendre[0, 0] = cos_polar * 0.0 + 0.5 / np.sqrt(np.pi)
    for m in range(1, order + 1):
        legendre[m, m] = -np.sqrt((2.0 * m + 1.0) / (2.0 * m)) * sin_polar * legendre[m - 1, m - 1]
    for m in range(order):
        legendre[m + 1, m] = np.sqrt(2.0 * m + 3.0) * cos_polar * legendre[m, m]
    for m in range(order + 1):
        for l in range(m + 2, order + 1):
            factor = np.sqrt((4.0 * l * l - 1.0) / (l * l - m * m))
            backward = np.sqrt(((l - 1.0) ** 2 - m * m) / (4.0 * (l - 1.0) ** 2 - 1.0))
            legendre[l, m] = factor * (
                cos_polar * legendre[l - 1, m] - backward * legendre[l - 2, m]
            )
    columns = []
    for l in range(order + 1):
        for m in range(-l, l + 1):
            if m > 0:
                columns.append(np.sqrt(2.0) * legendre[l, m] * np.cos(m * az_grid))
            elif m < 0:
                columns.append(np.sqrt(2.0) * legendre[l, -m] * np.sin(-m * az_grid))
            else:
                columns.append(legendre[l, 0])
    return np.stack(columns, axis=1)


def kernel_block(pieces):
    points, forces, centers = pieces
    panels = centers.shape[1] // 3
    source = points.astype(jnp.float32)
    strength = forces.astype(jnp.float32)
    spots = centers.reshape(centers.shape[0], 3, panels)
    offset = [spots[:, a, :, None] - source[:, a, None, :] for a in range(3)]
    radius_sq = offset[0] * offset[0] + offset[1] * offset[1] + offset[2] * offset[2] + soft_core
    inverse = lax.rsqrt(radius_sq)
    inverse_cube = inverse * inverse * inverse
    along = (
        offset[0] * strength[:, 0, None, :]
        + offset[1] * strength[:, 1, None, :]
        + offset[2] * strength[:, 2, None, :]
    )
    parts = [
        jnp.sum(strength[:, a, None, :] * inverse + offset[a] * along * inverse_cube, axis=2)
        for a in range(3)
    ]
    return jnp.stack(parts, axis=1).reshape(centers.shape[0], 3 * panels) * stokes_scale


def stokes_rows(points, forces, centers, block):
    total = points.shape[0]
    width = math.gcd(total, block)
    groups = total // width
    result = lax.map(
        kernel_block,
        (
            points.reshape(groups, width, 3, points.shape[2]),
            forces.reshape(groups, width, 3, forces.shape[2]),
            centers.reshape(groups, width, centers.shape[1]),
        ),
    )
    return result.reshape(total, centers.shape[1])


def local(
    shape_coef,
    force_coef,
    near_cell,
    near_dest,
    near_slot,
    panel_centers,
    near_blocks,
    near_pick,
    src_basis,
    far_couple,
    far_src,
    far_rank,
    tgt_basis,
    cluster_slot,
):
    walls = lax.axis_size(WALL)
    near_count = near_cell.shape[0]
    cluster_count = panel_centers.shape[0]
    cap = max(2, 2 * near_count // walls)
    harmonic = jnp.asarray(harmonics(ORDER), jnp.float32).astype(jnp.bfloat16)
    surface = jnp.einsum(
        "qs,asc->aqc", harmonic, shape_coef, preferred_element_type=jnp.float32
    ).astype(jnp.bfloat16)
    points = jnp.transpose(jnp.take(surface, near_cell, axis=2), (2, 0, 1))
    picked = jnp.take(force_coef, near_cell, axis=2)
    forces = jnp.einsum("qs,asn->naq", harmonic, picked, preferred_element_type=jnp.float32).astype(
        jnp.bfloat16
    )
    dest_hits = (near_dest[:, None] == jnp.arange(walls, dtype=jnp.int32)[None, :]).astype(
        jnp.int32
    )
    position = jnp.sum(jnp.cumsum(dest_hits, axis=0) * dest_hits, axis=1) - 1
    slot_index = near_dest * cap + position
    id_buffer = (
        jnp.full((walls * cap,), -1, jnp.int32).at[slot_index].set(near_slot).reshape(walls, cap)
    )
    payload = jnp.concatenate([points, forces], axis=1)
    pay_buffer = (
        jnp.zeros((walls * cap, 6, payload.shape[2]), jnp.bfloat16).at[slot_index].set(payload)
    )
    pay_buffer = pay_buffer.reshape(walls, cap, 6, payload.shape[2])
    recv_pay = lax.all_to_all(pay_buffer, WALL, split_axis=0, concat_axis=0, tiled=True)
    recv_ids = lax.all_to_all(id_buffer, WALL, split_axis=0, concat_axis=0, tiled=True)
    slot_count = recv_pay.shape[0] * recv_pay.shape[1]
    flat_ids = recv_ids.reshape(slot_count)
    centers = jnp.take(panel_centers, jnp.maximum(flat_ids, 0), axis=0)
    flat_pay = recv_pay.reshape(slot_count, 6, recv_pay.shape[3])
    velocity = stokes_rows(flat_pay[:, :3], flat_pay[:, 3:], centers, 8)
    recv_vel, recv_ids = (
        velocity.reshape(recv_pay.shape[0], recv_pay.shape[1], centers.shape[1]),
        recv_ids,
    )
    owner_hits = (
        recv_ids[:, :, None] == jnp.arange(cluster_count, dtype=jnp.int32)[None, None, :]
    ).astype(jnp.float32)
    wall_rhs = -jnp.einsum("wkc,wkp->cp", owner_hits, recv_vel, precision=lax.Precision.HIGHEST)
    source_rows = jnp.take(cluster_slot, far_src, axis=0)
    rank_size = far_couple.shape[2]
    levels = jnp.arange(rank_size, dtype=jnp.int32)
    rank_keep = (levels[None, None, :, None] < far_rank[:, :, None, None]) & (
        levels[None, None, None, :] < far_rank[:, :, None, None]
    )
    masked = jnp.where(rank_keep, far_couple, jnp.zeros_like(far_couple))
    density = wall_rhs
    for step in range(ITERS):
        density_low = density.astype(jnp.bfloat16)
        neighbor = shifted(density_low, WALL, 1)
        paired = jnp.stack([density_low, jnp.take(neighbor, near_pick, axis=0)], axis=1)
        near_term = jnp.einsum(
            "cbij,cbj->ci", near_blocks, paired, preferred_element_type=jnp.float32
        )
        coefficients = jnp.einsum("cpr,cp->cr", src_basis, density, precision=lax.Precision.HIGHEST)
        coef_table = whole_of(coefficients, CELLS_WALL, (0, 1, 2, 3), 0)
        gathered = jnp.take(coef_table, source_rows, axis=0)
        mixed_rank = jnp.einsum("cbij,cbj->ci", masked, gathered, precision=lax.Precision.HIGHEST)
        far_term = jnp.einsum("cr,crp->cp", mixed_rank, tgt_basis, precision=lax.Precision.HIGHEST)
        density = wall_rhs - near_term - far_term
    return (surface, density)


def solution(mesh):
    finer = Mesh(mesh.devices.reshape(4, 4, 32, 2), ("cells_0", "cells_1", "wall_0", "wall_1"))
    return jax.shard_map(
        local,
        mesh=finer,
        in_specs=(
            P(None, None, CELLS_WALL),
            P(None, None, CELLS_WALL),
            P(CELLS_WALL),
            P(CELLS_WALL),
            P(CELLS_WALL),
            P(CELLS_WALL, None),
            P(CELLS_WALL, None, None, None),
            P(CELLS_WALL),
            P(CELLS_WALL, None, None),
            P(CELLS_WALL, None, None, None),
            P(CELLS_WALL, None),
            P(CELLS_WALL, None),
            P(CELLS_WALL, None, None),
            P(),
        ),
        out_specs=(P(None, None, CELLS_WALL), P(CELLS_WALL, None)),
        check_vma=False,
    )
```

profile of v0, /device:TPU:1, one launch (start us, length us, event | category | flops | bytes accessed | tf_op | source)
XLA Modules:
  0.0 453.3 jit_solution(336563983463933594)
XLA Ops:
  4.8 30.4 %all-to-all-start = ((s32[64,1,2]{2,1,0:T(1,128)}), s32[64,1,2]{2,1,0:T(1,128)S(1)}, u32[]{:S(2)}, u32[]{:S(2)}) async-start(s32[64,1,2]{2,1,0:T(1,128)} %bitcast.20), calls=%async_computation | async-start | bytes 65536 | tf_op jit(solution)/shard_map/all_to_all | solution.py:157
  40.9 2.7 copy.82
  49.5 8.0 %all-to-all-done = s32[64,1,2]{2,1,0:T(1,128)S(1)} async-done(((s32[64,1,2]{2,1,0:T(1,128)}), s32[64,1,2]{2,1,0:T(1,128)S(1)}, u32[]{:S(2)}, u32[]{:S(2)}) %all-to-all-start) | async-done | bytes 544 | tf_op jit(solution)/shard_map/all_to_all | solution.py:157
  57.4 14.4 %all-to-all-start.1 = ((bf16[64,2,6,578]{3,1,2,0:T(2,128)(2,1)}), bf16[64,2,6,578]{3,1,2,0:T(2,128)(2,1)S(1)}, u32[]{:S(2)}, u32[]{:S(2)}) async-start(bf16[64,2,6,578]{3,1,2,0:T(2,128)(2,1)} %copy.87), calls=%async_computation.1 | async-start | bytes 1966080 | tf_op jit(solution)/shard_map/all_to_all | solution.py:156
  78.4 95.5 %all-to-all-done.1 = bf16[64,2,6,578]{3,1,2,0:T(2,128)(2,1)S(1)} async-done(((bf16[64,2,6,578]{3,1,2,0:T(2,128)(2,1)}), bf16[64,2,6,578]{3,1,2,0:T(2,128)(2,1)S(1)}, u32[]{:S(2)}, u32[]{:S(2)}) %all-to-all-start.1) | async-done | bytes 887840 | tf_op jit(solution)/shard_map/all_to_all | solution.py:156
  175.4 107.6 %while.10 = (s32[]{:T(128)}, f32[16,8,384]{2,1,0:T(8,128)}, bf16[16,8,3,578]{3,1,0,2:T(8,128)(2,1)S(1)}, f32[16,8,384]{2,1,0:T(8,128)}, bf16[16,8,3,578]{3,1,0,2:T(8,128)(2,1)S(1)}, /*index=5*/s32[]{:T(128)}) while((s32[]{:T(128)}, f32[16,8,384]{2,1,0:T(8,128)}, bf16[16,8,3,578]{3,1,0,2:T(8,128)(2,1)S(1)}, f32[16,8,384]{2,1,0:T(8,128)}, ...), condition=%wide.region_8.9_spmd, body=%wide.region_4.8_spmd.sunk | while | flops 18381920 | bytes 819737 | solution.py:103
  177.0 4.6 %fusion.65 = (f32[8,128]{1,0:T(8,128)S(1)}, f32[8,128]{1,0:T(8,128)S(1)}, f32[8,128]{1,0:T(8,128)S(1)}) fusion(f32[8,578]{0,1:T(8,128)S(1)} %get-tuple-element.120, f32[8,578]{0,1:T(8,128)S(1)} %get-tuple-element.121, f32[8,578]{0,1:T(8,128)S(1)} %get-tuple-element.123, f32[8,128]{1,0:T(8,128)S(1)} %get-tuple-element.124, ...), kind=kLoop, calls=%fused_computation.28.clone.1 | loop fusion | flops 18344960 | bytes 135552 | tf_op jit(solution)/shard_map/while/body/eval_jaxpr/reduce_sum | solution.py:93
  183.7 4.6 %fusion.65 = (f32[8,128]{1,0:T(8,128)S(1)}, f32[8,128]{1,0:T(8,128)S(1)}, f32[8,128]{1,0:T(8,128)S(1)}) fusion(f32[8,578]{0,1:T(8,128)S(1)} %get-tuple-element.120, f32[8,578]{0,1:T(8,128)S(1)} %get-tuple-element.121, f32[8,578]{0,1:T(8,128)S(1)} %get-tuple-element.123, f32[8,128]{1,0:T(8,128)S(1)} %get-tuple-element.124, ...), kind=kLoop, calls=%fused_computation.28.clone.1 | loop fusion | flops 18344960 | bytes 135552 | tf_op jit(solution)/shard_map/while/body/eval_jaxpr/reduce_sum | solution.py:93
  190.4 4.6 %fusion.65 = (f32[8,128]{1,0:T(8,128)S(1)}, f32[8,128]{1,0:T(8,128)S(1)}, f32[8,128]{1,0:T(8,128)S(1)}) fusion(f32[8,578]{0,1:T(8,128)S(1)} %get-tuple-element.120, f32[8,578]{0,1:T(8,128)S(1)} %get-tuple-element.121, f32[8,578]{0,1:T(8,128)S(1)} %get-tuple-element.123, f32[8,128]{1,0:T(8,128)S(1)} %get-tuple-element.124, ...), kind=kLoop, calls=%fused_computation.28.clone.1 | loop fusion | flops 18344960 | bytes 135552 | tf_op jit(solution)/shard_map/while/body/eval_jaxpr/reduce_sum | solution.py:93
  197.2 4.6 %fusion.65 = (f32[8,128]{1,0:T(8,128)S(1)}, f32[8,128]{1,0:T(8,128)S(1)}, f32[8,128]{1,0:T(8,128)S(1)}) fusion(f32[8,578]{0,1:T(8,128)S(1)} %get-tuple-element.120, f32[8,578]{0,1:T(8,128)S(1)} %get-tuple-element.121, f32[8,578]{0,1:T(8,128)S(1)} %get-tuple-element.123, f32[8,128]{1,0:T(8,128)S(1)} %get-tuple-element.124, ...), kind=kLoop, calls=%fused_computation.28.clone.1 | loop fusion | flops 18344960 | bytes 135552 | tf_op jit(solution)/shard_map/while/body/eval_jaxpr/reduce_sum | solution.py:93
  203.9 4.6 %fusion.65 = (f32[8,128]{1,0:T(8,128)S(1)}, f32[8,128]{1,0:T(8,128)S(1)}, f32[8,128]{1,0:T(8,128)S(1)}) fusion(f32[8,578]{0,1:T(8,128)S(1)} %get-tuple-element.120, f32[8,578]{0,1:T(8,128)S(1)} %get-tuple-element.121, f32[8,578]{0,1:T(8,128)S(1)} %get-tuple-element.123, f32[8,128]{1,0:T(8,128)S(1)} %get-tuple-element.124, ...), kind=kLoop, calls=%fused_computation.28.clone.1 | loop fusion | flops 18344960 | bytes 135552 | tf_op jit(solution)/shard_map/while/body/eval_jaxpr/reduce_sum | solution.py:93
  210.6 4.6 %fusion.65 = (f32[8,128]{1,0:T(8,128)S(1)}, f32[8,128]{1,0:T(8,128)S(1)}, f32[8,128]{1,0:T(8,128)S(1)}) fusion(f32[8,578]{0,1:T(8,128)S(1)} %get-tuple-element.120, f32[8,578]{0,1:T(8,128)S(1)} %get-tuple-element.121, f32[8,578]{0,1:T(8,128)S(1)} %get-tuple-element.123, f32[8,128]{1,0:T(8,128)S(1)} %get-tuple-element.124, ...), kind=kLoop, calls=%fused_computation.28.clone.1 | loop fusion | flops 18344960 | bytes 135552 | tf_op jit(solution)/shard_map/while/body/eval_jaxpr/reduce_sum | solution.py:93
  217.3 4.6 %fusion.65 = (f32[8,128]{1,0:T(8,128)S(1)}, f32[8,128]{1,0:T(8,128)S(1)}, f32[8,128]{1,0:T(8,128)S(1)}) fusion(f32[8,578]{0,1:T(8,128)S(1)} %get-tuple-element.120, f32[8,578]{0,1:T(8,128)S(1)} %get-tuple-element.121, f32[8,578]{0,1:T(8,128)S(1)} %get-tuple-element.123, f32[8,128]{1,0:T(8,128)S(1)} %get-tuple-element.124, ...), kind=kLoop, calls=%fused_computation.28.clone.1 | loop fusion | flops 18344960 | bytes 135552 | tf_op jit(solution)/shard_map/while/body/eval_jaxpr/reduce_sum | solution.py:93
  224.1 4.6 %fusion.65 = (f32[8,128]{1,0:T(8,128)S(1)}, f32[8,128]{1,0:T(8,128)S(1)}, f32[8,128]{1,0:T(8,128)S(1)}) fusion(f32[8,578]{0,1:T(8,128)S(1)} %get-tuple-element.120, f32[8,578]{0,1:T(8,128)S(1)} %get-tuple-element.121, f32[8,578]{0,1:T(8,128)S(1)} %get-tuple-element.123, f32[8,128]{1,0:T(8,128)S(1)} %get-tuple-element.124, ...), kind=kLoop, calls=%fused_computation.28.clone.1 | loop fusion | flops 18344960 | bytes 135552 | tf_op jit(solution)/shard_map/while/body/eval_jaxpr/reduce_sum | solution.py:93
  230.8 4.6 %fusion.65 = (f32[8,128]{1,0:T(8,128)S(1)}, f32[8,128]{1,0:T(8,128)S(1)}, f32[8,128]{1,0:T(8,128)S(1)}) fusion(f32[8,578]{0,1:T(8,128)S(1)} %get-tuple-element.120, f32[8,578]{0,1:T(8,128)S(1)} %get-tuple-element.121, f32[8,578]{0,1:T(8,128)S(1)} %get-tuple-element.123, f32[8,128]{1,0:T(8,128)S(1)} %get-tuple-element.124, ...), kind=kLoop, calls=%fused_computation.28.clone.1 | loop fusion | flops 18344960 | bytes 135552 | tf_op jit(solution)/shard_map/while/body/eval_jaxpr/reduce_sum | solution.py:93
  237.5 4.6 %fusion.65 = (f32[8,128]{1,0:T(8,128)S(1)}, f32[8,128]{1,0:T(8,128)S(1)}, f32[8,128]{1,0:T(8,128)S(1)}) fusion(f32[8,578]{0,1:T(8,128)S(1)} %get-tuple-element.120, f32[8,578]{0,1:T(8,128)S(1)} %get-tuple-element.121, f32[8,578]{0,1:T(8,128)S(1)} %get-tuple-element.123, f32[8,128]{1,0:T(8,128)S(1)} %get-tuple-element.124, ...), kind=kLoop, calls=%fused_computation.28.clone.1 | loop fusion | flops 18344960 | bytes 135552 | tf_op jit(solution)/shard_map/while/body/eval_jaxpr/reduce_sum | solution.py:93
  244.2 4.6 %fusion.65 = (f32[8,128]{1,0:T(8,128)S(1)}, f32[8,128]{1,0:T(8,128)S(1)}, f32[8,128]{1,0:T(8,128)S(1)}) fusion(f32[8,578]{0,1:T(8,128)S(1)} %get-tuple-element.120, f32[8,578]{0,1:T(8,128)S(1)} %get-tuple-element.121, f32[8,578]{0,1:T(8,128)S(1)} %get-tuple-element.123, f32[8,128]{1,0:T(8,128)S(1)} %get-tuple-element.124, ...), kind=kLoop, calls=%fused_computation.28.clone.1 | loop fusion | flops 18344960 | bytes 135552 | tf_op jit(solution)/shard_map/while/body/eval_jaxpr/reduce_sum | solution.py:93
  251.0 4.6 %fusion.65 = (f32[8,128]{1,0:T(8,128)S(1)}, f32[8,128]{1,0:T(8,128)S(1)}, f32[8,128]{1,0:T(8,128)S(1)}) fusion(f32[8,578]{0,1:T(8,128)S(1)} %get-tuple-element.120, f32[8,578]{0,1:T(8,128)S(1)} %get-tuple-element.121, f32[8,578]{0,1:T(8,128)S(1)} %get-tuple-element.123, f32[8,128]{1,0:T(8,128)S(1)} %get-tuple-element.124, ...), kind=kLoop, calls=%fused_computation.28.clone.1 | loop fusion | flops 18344960 | bytes 135552 | tf_op jit(solution)/shard_map/while/body/eval_jaxpr/reduce_sum | solution.py:93
  257.7 4.6 %fusion.65 = (f32[8,128]{1,0:T(8,128)S(1)}, f32[8,128]{1,0:T(8,128)S(1)}, f32[8,128]{1,0:T(8,128)S(1)}) fusion(f32[8,578]{0,1:T(8,128)S(1)} %get-tuple-element.120, f32[8,578]{0,1:T(8,128)S(1)} %get-tuple-element.121, f32[8,578]{0,1:T(8,128)S(1)} %get-tuple-element.123, f32[8,128]{1,0:T(8,128)S(1)} %get-tuple-element.124, ...), kind=kLoop, calls=%fused_computation.28.clone.1 | loop fusion | flops 18344960 | bytes 135552 | tf_op jit(solution)/shard_map/while/body/eval_jaxpr/reduce_sum | solution.py:93
  264.4 4.6 %fusion.65 = (f32[8,128]{1,0:T(8,128)S(1)}, f32[8,128]{1,0:T(8,128)S(1)}, f32[8,128]{1,0:T(8,128)S(1)}) fusion(f32[8,578]{0,1:T(8,128)S(1)} %get-tuple-element.120, f32[8,578]{0,1:T(8,128)S(1)} %get-tuple-element.121, f32[8,578]{0,1:T(8,128)S(1)} %get-tuple-element.123, f32[8,128]{1,0:T(8,128)S(1)} %get-tuple-element.124, ...), kind=kLoop, calls=%fused_computation.28.clone.1 | loop fusion | flops 18344960 | bytes 135552 | tf_op jit(solution)/shard_map/while/body/eval_jaxpr/reduce_sum | solution.py:93
  271.2 4.6 %fusion.65 = (f32[8,128]{1,0:T(8,128)S(1)}, f32[8,128]{1,0:T(8,128)S(1)}, f32[8,128]{1,0:T(8,128)S(1)}) fusion(f32[8,578]{0,1:T(8,128)S(1)} %get-tuple-element.120, f32[8,578]{0,1:T(8,128)S(1)} %get-tuple-element.121, f32[8,578]{0,1:T(8,128)S(1)} %get-tuple-element.123, f32[8,128]{1,0:T(8,128)S(1)} %get-tuple-element.124, ...), kind=kLoop, calls=%fused_computation.28.clone.1 | loop fusion | flops 18344960 | bytes 135552 | tf_op jit(solution)/shard_map/while/body/eval_jaxpr/reduce_sum | solution.py:93
  277.9 4.6 %fusion.65 = (f32[8,128]{1,0:T(8,128)S(1)}, f32[8,128]{1,0:T(8,128)S(1)}, f32[8,128]{1,0:T(8,128)S(1)}) fusion(f32[8,578]{0,1:T(8,128)S(1)} %get-tuple-element.120, f32[8,578]{0,1:T(8,128)S(1)} %get-tuple-element.121, f32[8,578]{0,1:T(8,128)S(1)} %get-tuple-element.123, f32[8,128]{1,0:T(8,128)S(1)} %get-tuple-element.124, ...), kind=kLoop, calls=%fused_computation.28.clone.1 | loop fusion | flops 18344960 | bytes 135552 | tf_op jit(solution)/shard_map/while/body/eval_jaxpr/reduce_sum | solution.py:93
  286.0 7.7 %all-gather.8 = f32[4,2,16]{2,1,0:T(2,128)S(1)} all-gather(f32[1,2,16]{2,1,0:T(2,128)S(1)} %bitcast.182), channel_id=2, replica_groups=mesh['cells_0'=4,'cells_1'=4,'wall_0'=32,'wall_1'=2] {'cells_0'}, dimensions={0}, use_global_device_ids=true | all-gather | bytes 640 | tf_op jit(solution)/shard_map/all_gather | solution.py:34
  293.7 4.2 collective-permute-start
  297.9 9.6 %all-gather.1 = f32[16,2,16]{2,1,0:T(2,128)S(1)} all-gather(f32[4,2,16]{2,1,0:T(2,128)S(1)} %all-gather.8), channel_id=3, replica_groups=mesh['cells_0'=4,'cells_1'=4,'wall_0'=32,'wall_1'=2] {'cells_1'}, dimensions={0}, use_global_device_ids=true | all-gather | bytes 2560 | tf_op jit(solution)/shard_map/all_gather | solution.py:34
  307.5 44.8 %all-gather.2 = f32[128,4,2,16]{3,1,2,0:T(4,128)S(1)} all-gather(f32[4,4,2,16]{3,1,2,0:T(4,128)S(1)} %copy.92), channel_id=4, replica_groups=mesh['cells_0'=4,'cells_1'=4,'wall_0'=32,'wall_1'=2] {'wall_0'}, dimensions={0}, use_global_device_ids=true | all-gather | bytes 67584 | tf_op jit(solution)/shard_map/all_gather | solution.py:34
  352.4 16.1 %all-gather.3 = f32[64,4,4,2,16]{4,1,0,3,2:T(4,128)S(1)} all-gather(f32[32,4,4,2,16]{4,1,0,3,2:T(4,128)S(1)} %bitcast.165), channel_id=5, replica_groups=mesh['cells_0'=4,'cells_1'=4,'wall_0'=32,'wall_1'=2] {'wall_1'}, dimensions={0}, use_global_device_ids=true | all-gather | bytes 196608 | tf_op jit(solution)/shard_map/all_gather | solution.py:34
  371.9 5.4 %all-gather.9 = f32[4,2,16]{2,1,0:T(2,128)S(1)} all-gather(f32[1,2,16]{2,1,0:T(2,128)S(1)} %bitcast.181), channel_id=6, replica_groups=mesh['cells_0'=4,'cells_1'=4,'wall_0'=32,'wall_1'=2] {'cells_0'}, dimensions={0}, use_global_device_ids=true | all-gather | bytes 640 | tf_op jit(solution)/shard_map/all_gather | solution.py:34
  377.3 3.3 collective-permute-start.1
  380.6 9.1 %all-gather.5 = f32[16,2,16]{2,1,0:T(2,128)S(1)} all-gather(f32[4,2,16]{2,1,0:T(2,128)S(1)} %all-gather.9), channel_id=7, replica_groups=mesh['cells_0'=4,'cells_1'=4,'wall_0'=32,'wall_1'=2] {'cells_1'}, dimensions={0}, use_global_device_ids=true | all-gather | bytes 2560 | tf_op jit(solution)/shard_map/all_gather | solution.py:34
  389.8 41.9 %all-gather.6 = f32[128,4,2,16]{3,1,2,0:T(4,128)S(1)} all-gather(f32[4,4,2,16]{3,1,2,0:T(4,128)S(1)} %copy.96), channel_id=8, replica_groups=mesh['cells_0'=4,'cells_1'=4,'wall_0'=32,'wall_1'=2] {'wall_0'}, dimensions={0}, use_global_device_ids=true | all-gather | bytes 67584 | tf_op jit(solution)/shard_map/all_gather | solution.py:34
  431.8 17.8 %all-gather.7 = f32[64,4,4,2,16]{4,1,0,3,2:T(4,128)S(1)} all-gather(f32[32,4,4,2,16]{4,1,0,3,2:T(4,128)S(1)} %bitcast.166), channel_id=9, replica_groups=mesh['cells_0'=4,'cells_1'=4,'wall_0'=32,'wall_1'=2] {'wall_1'}, dimensions={0}, use_global_device_ids=true | all-gather | bytes 196608 | tf_op jit(solution)/shard_map/all_gather | solution.py:34
  (265 shorter events, 67.0 us)
Async XLA Ops:
  0.6 370.7 %copy-start = (bf16[2,2,384,384]{3,2,1,0:T(8,128)(2,1)S(1)}, bf16[2,2,384,384]{3,2,1,0:T(8,128)(2,1)}, u32[]{:S(2)}) copy-start(bf16[2,2,384,384]{3,2,1,0:T(8,128)(2,1)} %param.27) | copy-start | bytes 3538948
  0.6 38.3 %copy-start.3 = (bf16[578,289,1]{0,1,2:T(8,128)(2,1)S(1)}, bf16[578,289,1]{0,1,2:T(8,128)(2,1)}, u32[]{:S(2)}) copy-start(bf16[578,289,1]{0,1,2:T(8,128)(2,1)} %constant.134) | copy-start | bytes 1002256
  4.8 52.7 %all-to-all-start = ((s32[64,1,2]{2,1,0:T(1,128)}), s32[64,1,2]{2,1,0:T(1,128)S(1)}, u32[]{:S(2)}, u32[]{:S(2)}) async-start(s32[64,1,2]{2,1,0:T(1,128)} %bitcast.20), calls=%async_computation | async-start | bytes 65536 | tf_op jit(solution)/shard_map/all_to_all | solution.py:157
  36.5 2.8 copy-start.12
  49.4 22.5 %copy-start.8 = (s32[2,8]{1,0:T(2,128)S(1)}, s32[2,8]{1,0:T(2,128)}, u32[]{:S(2)}) copy-start(s32[2,8]{1,0:T(2,128)} %param.31) | copy-start | bytes 196
  49.4 22.6 %copy-start.2 = (s32[2048]{0:T(1024)S(1)}, s32[2048]{0:T(1024)}, u32[]{:S(2)}) copy-start(s32[2048]{0:T(1024)} %param.34) | copy-start | bytes 24580
  49.4 23.9 %copy-start.14 = (s32[2]{0:T(128)S(1)}, s32[2]{0:T(128)}, u32[]{:S(2)}) copy-start(s32[2]{0:T(128)} %param.28) | copy-start | bytes 28
  49.4 25.6 %copy-start.11 = (s32[2,8]{1,0:T(2,128)S(1)}, s32[2,8]{1,0:T(2,128)}, u32[]{:S(2)}) copy-start(s32[2,8]{1,0:T(2,128)} %param.32) | copy-start | bytes 196
  49.4 26.8 %copy-start.1 = (f32[2,384]{1,0:T(2,128)S(1)}, f32[2,384]{1,0:T(2,128)}, u32[]{:S(2)}) copy-start(f32[2,384]{1,0:T(2,128)} %param.26) | copy-start | bytes 9220
  57.4 116.5 %all-to-all-start.1 = ((bf16[64,2,6,578]{3,1,2,0:T(2,128)(2,1)}), bf16[64,2,6,578]{3,1,2,0:T(2,128)(2,1)S(1)}, u32[]{:S(2)}, u32[]{:S(2)}) async-start(bf16[64,2,6,578]{3,1,2,0:T(2,128)(2,1)} %copy.87), calls=%async_computation.1 | async-start | bytes 1966080 | tf_op jit(solution)/shard_map/all_to_all | solution.py:156
  293.7 76.8 %collective-permute-start = (bf16[2,384]{1,0:T(2,128)(2,1)S(1)}, bf16[2,384]{1,0:T(2,128)(2,1)S(1)}, u32[]{:S(2)}, u32[]{:S(2)}) collective-permute-start(bf16[2,384]{1,0:T(2,128)(2,1)S(1)} %get-tuple-element.72), channel_id=1, source_target_pairs={{0,1},{1,2},{2,3},{3,4},{4,5},{5,6},{6,7},{7,8},{8,9},{9,10},{10,1... | collective-permute-start | bytes 4616 | tf_op jit(solution)/shard_map/ppermute | solution.py:22
  368.5 0.9 copy-start.6
  368.5 1.4 copy-start.7
  368.5 1.5 copy-start.10
  368.5 1.5 copy-start.13
  368.5 1.9 copy-start.5
  368.5 2.7 copy-start.9
  368.5 3.2 copy-start.4
  377.3 74.2 %collective-permute-start.1 = (bf16[2,384]{1,0:T(2,128)(2,1)S(1)}, bf16[2,384]{1,0:T(2,128)(2,1)S(1)}, u32[]{:S(2)}, u32[]{:S(2)}) collective-permute-start(bf16[2,384]{1,0:T(2,128)(2,1)S(1)} %get-tuple-element.55), channel_id=1, source_target_pairs={{0,1},{1,2},{2,3},{3,4},{4,5},{5,6},{6,7},{7,8},{8,9},{9,10},{10,1... | collective-permute-start | bytes 4616 | tf_op jit(solution)/shard_map/ppermute | solution.py:22
where the time goes:
time: 455 us; the launch traced here: 453 us
  blocking collectives  152 us (33%)
  waiting for transfers between devices  104 us (23%)
  other arithmetic  94.2 us (21%)
  starting transfers between devices  52.3 us (11%)
  local copies, waits for them, and re-layouts  43.3 us (10%)
  matrix products  5.73 us (1%)
    all_gather x8, blocking collectives, gather_in_order(): pieces = lax.all_gather(pieces, axes[k])  152 us
    all_to_all x1, waiting for transfers between devices, local(): lax.all_to_all(pay_buffer, WALL, split_axis=0, concat_axis=0, tiled=True)  95.5 us
    reduce_sum x16, other arithmetic, kernel_block(): jnp.sum(strength[:, a, None, :] * inverse + offset[a] * along * inverse_c...  73.6 us
    all_to_all x1, starting transfers between devices, local(): lax.all_to_all(id_buffer, WALL, split_axis=0, concat_axis=0, tiled=True)  30.4 us
    all_to_all x1, starting transfers between devices, local(): lax.all_to_all(pay_buffer, WALL, split_axis=0, concat_axis=0, tiled=True)  14.4 us
    reshape x16, local copies, waits for them, and re-layouts, kernel_block(): spots = centers.reshape(centers.shape[0], 3, panels)  11.3 us
    dynamic_update_slice x16, other arithmetic, stokes_rows(): lax.map(kernel_block, (points.reshape(groups, width, 3, points.shape[2]),...  9.69 us
  transfers between devices with their start and end apart: 4, of which 2 were waited for; matrix products, arithmetic and copies ran while one was open for 5% of the time, Pallas kernels for 0%

commit v1 on v0

v1 whole, which is shorter than its diff:
```python
import functools
import math

import jax
import jax.numpy as jnp
import numpy as np
from jax import lax
from jax.experimental import pallas as pl
from jax.experimental.pallas import tpu as pltpu
from jax.sharding import Mesh
from jax.sharding import PartitionSpec as P

ORDER = 16
ITERS = 2
WALL = ("wall_0", "wall_1")
CELLS = ("cells_0", "cells_1")
CELLS_WALL = ("cells_0", "cells_1", "wall_0", "wall_1")

soft_core = 0.25
stokes_scale = 1.0 / (8.0 * math.pi)
LANES = 128
PANELS = 128
f32 = jnp.float32
bf16 = jnp.bfloat16
VMEM = pl.BlockSpec(memory_space=pltpu.VMEM)
SMEM = pl.BlockSpec(memory_space=pltpu.SMEM)


def shifted(array, axis, by):
    devices = lax.axis_size(axis)
    return lax.ppermute(array, axis, [(i, (i + by) % devices) for i in range(devices)])


def harmonics(order):
    lat_count = order + 1
    polar_angle = np.pi * (np.arange(lat_count) + 0.5) / lat_count
    azimuth = np.pi * np.arange(2 * lat_count) / lat_count
    cos_polar = np.repeat(np.cos(polar_angle), 2 * lat_count)
    sin_polar = np.repeat(np.sin(polar_angle), 2 * lat_count)
    az_grid = np.tile(azimuth, lat_count)
    legendre = {}
    legendre[0, 0] = cos_polar * 0.0 + 0.5 / np.sqrt(np.pi)
    for m in range(1, order + 1):
        legendre[m, m] = -np.sqrt((2.0 * m + 1.0) / (2.0 * m)) * sin_polar * legendre[m - 1, m - 1]
    for m in range(order):
        legendre[m + 1, m] = np.sqrt(2.0 * m + 3.0) * cos_polar * legendre[m, m]
    for m in range(order + 1):
        for l in range(m + 2, order + 1):
            factor = np.sqrt((4.0 * l * l - 1.0) / (l * l - m * m))
            backward = np.sqrt(((l - 1.0) ** 2 - m * m) / (4.0 * (l - 1.0) ** 2 - 1.0))
            legendre[l, m] = factor * (
                cos_polar * legendre[l - 1, m] - backward * legendre[l - 2, m]
            )
    columns = []
    for l in range(order + 1):
        for m in range(-l, l + 1):
            if m > 0:
                columns.append(np.sqrt(2.0) * legendre[l, m] * np.cos(m * az_grid))
            elif m < 0:
                columns.append(np.sqrt(2.0) * legendre[l, -m] * np.sin(-m * az_grid))
            else:
                columns.append(legendre[l, 0])
    return np.stack(columns, axis=1)


def dot_nn(a, b):
    return lax.dot_general(a, b, (((1,), (0,)), ((), ())), preferred_element_type=f32)


def dot_nt(a, b):
    return lax.dot_general(a, b, (((1,), (1,)), ((), ())), preferred_element_type=f32)


def dot_tn(a, b):
    return lax.dot_general(a, b, (((0,), (0,)), ((), ())), preferred_element_type=f32)


def split3(value):
    high = value.astype(bf16).astype(f32)
    rest = value - high
    middle = rest.astype(bf16).astype(f32)
    return high, middle, rest - middle


def sources_kernel(cell_ref, shape_ref, force_ref, grid_ref, out_ref):
    rows = out_ref.shape[1]
    cells = shape_ref.shape[2]
    pick = (lax.broadcasted_iota(jnp.int32, (rows, cells), 1) == cell_ref[...]).astype(bf16)
    for base, ref in ((0, shape_ref), (3, force_ref)):
        for a in range(3):
            coefs = dot_nt(pick, ref[a]).astype(bf16)
            out_ref[base + a] = dot_nn(coefs, grid_ref[...]).astype(bf16)


def near_sources(near_cell, shape_coef, force_coef, grid):
    rows = near_cell.shape[0]
    return pl.pallas_call(
        sources_kernel,
        out_shape=jax.ShapeDtypeStruct((6, rows, grid.shape[1]), bf16),
        in_specs=[VMEM] * 4,
        out_specs=VMEM,
        cost_estimate=pl.CostEstimate(flops=200_000_000, bytes_accessed=2_500_000, transcendentals=0),
        name="near_sources",
    )(near_cell.reshape(rows, 1), shape_coef, force_coef, grid)


def put(ref, k, value):
    rows = value.shape[0]
    for j in range(ref.shape[0]):
        ref[j, pl.ds(k * rows, rows), :] = value[:, j * LANES : (j + 1) * LANES]


def get(ref, r, rows):
    return jnp.concatenate(
        [ref[j, pl.ds(r, 16, stride=rows), :] for j in range(ref.shape[0])], axis=1
    )


def pairs_kernel(tcol_ref, trow_ref, src_ref, ctr_ref, out_ref, ysc, gsc, bsc, mom, xsc):
    rows, quads = src_ref.shape[1], src_ref.shape[2]
    walls, width = out_ref.shape
    pan = PANELS
    own = width // (3 * pan)
    clusters = walls * own
    lines = width // LANES
    y = [src_ref[a].astype(f32) for a in range(3)]
    f = [src_ref[3 + a].astype(f32) for a in range(3)]
    y2 = y[0] * y[0] + y[1] * y[1] + y[2] * y[2]
    yf = y[0] * f[0] + y[1] * f[1] + y[2] * f[2]
    for k in range(9):
        put(ysc, k, -2.0 * y[k % 3])
    for k, piece in enumerate(split3(y2)):
        put(ysc, 9 + k, piece)
    for k in range(12, 15):
        put(ysc, k, jnp.ones((rows, quads), f32))
    put(ysc, 15, jnp.zeros((rows, quads), f32))
    for b in range(3):
        put(gsc, b, f[b])
    put(gsc, 3, yf)
    for a in range(3):
        for b in range(3):
            put(gsc, 4 + 3 * a + b, y[a] * f[b])
        put(gsc, 13 + a, y[a] * yf)
    pick = (lax.broadcasted_iota(jnp.int32, (rows, clusters), 1) == tcol_ref[...]).astype(bf16)
    x = []
    for a in range(3):
        total = None
        spots = jnp.concatenate(
            [ctr_ref[pl.ds(3 * t + a, walls, stride=lines), :] for t in range(own)], axis=0
        )
        for i, piece in enumerate(split3(spots)):
            part = dot_nn(pick, piece.astype(bf16))
            bsc[pl.ds((3 * i + a) * rows, rows), :] = part
            total = part if total is None else total + part
        x.append(total)
        xsc[pl.ds(a * rows, rows), :] = total
    x2 = x[0] * x[0] + x[1] * x[1] + x[2] * x[2] + soft_core
    for k in range(9, 12):
        bsc[pl.ds(k * rows, rows), :] = jnp.ones((rows, pan), f32)
    for k, piece in enumerate(split3(x2)):
        bsc[pl.ds((12 + k) * rows, rows), :] = piece
    bsc[pl.ds(15 * rows, rows), :] = jnp.zeros((rows, pan), f32)

    def row(r, carry):
        yr = get(ysc, r, rows).astype(bf16)
        br = bsc[pl.ds(r, 16, stride=rows), :]
        g = get(gsc, r, rows)
        g_hi = g.astype(bf16)
        g_lo = (g - g_hi.astype(f32)).astype(bf16)
        rho2 = dot_tn(yr, br.astype(bf16))
        inverse = lax.rsqrt(rho2)
        cube = inverse * inverse * inverse
        c_hi = cube.astype(bf16)
        c_lo = (cube - c_hi.astype(f32)).astype(bf16)
        i_hi = inverse.astype(bf16)
        i_lo = (inverse - i_hi.astype(f32)).astype(bf16)
        first = dot_nn(jnp.concatenate([g_hi, g_lo], axis=0), c_hi)
        mom[pl.ds(r, 16, stride=rows), :] = first[:16] + first[16:] + dot_nn(g_hi, c_lo)
        plain = dot_nn(g_hi, i_hi) + dot_nn(g_hi, i_lo)
        mom[pl.ds(16 * rows + r, 8, stride=rows), :] = plain[:8]
        return carry

    lax.fori_loop(0, rows, row, 0, unroll=PAIR_UNROLL)
    x = [xsc[pl.ds(a * rows, rows), :] for a in range(3)]
    moment = [mom[pl.ds(c * rows, rows), :] for c in range(19)]
    common = x[0] * moment[0] + x[1] * moment[1] + x[2] * moment[2] - moment[3]
    drop = (lax.broadcasted_iota(jnp.int32, (clusters, rows), 0) == trow_ref[...]).astype(bf16)
    for a in range(3):
        local_part = x[0] * moment[4 + 3 * a] + x[1] * moment[5 + 3 * a] + x[2] * moment[6 + 3 * a]
        velocity = moment[16 + a] + x[a] * common - (local_part - moment[13 + a])
        velocity = velocity * (-stokes_scale)
        total = None
        for piece in split3(velocity):
            part = dot_nn(drop, piece.astype(bf16))
            total = part if total is None else total + part
        for t in range(own):
            out_ref[:, pl.ds((3 * t + a) * pan, pan)] = total[t * walls : (t + 1) * walls, :]


PAIR_UNROLL = 8


def pair_sums(target, sources, centers, walls):
    rows, quads = sources.shape[1:]
    width = centers.shape[0] * LANES // walls
    pan = PANELS
    return pl.pallas_call(
        pairs_kernel,
        out_shape=jax.ShapeDtypeStruct((walls, width), f32),
        in_specs=[VMEM] * 4,
        out_specs=VMEM,
        scratch_shapes=[
            pltpu.VMEM((quads // LANES, 16 * rows, LANES), f32),
            pltpu.VMEM((quads // LANES, 16 * rows, LANES), f32),
            pltpu.VMEM((16 * rows, pan), f32),
            pltpu.VMEM((24 * rows, pan), f32),
            pltpu.VMEM((3 * rows, pan), f32),
        ],
        cost_estimate=pl.CostEstimate(
            flops=1_000_000_000, bytes_accessed=1_000_000, transcendentals=5_000_000
        ),
        name="pair_sums",
    )(target.reshape(rows, 1), target.reshape(1, rows), sources, centers)


def coefs_of(density, basis_ref):
    parts = []
    for t in range(density.shape[0]):
        parts.append(
            lax.dot_general(
                density[t : t + 1, :],
                basis_ref[t],
                (((1,), (1,)), ((), ())),
                precision=lax.Precision.HIGHEST,
                preferred_element_type=f32,
            )
        )
    return jnp.concatenate(parts * (LANES // (len(parts) * parts[0].shape[1])), axis=1)


def start_kernel(recv_ref, basis_ref, rhs_ref, low_ref, coef_ref):
    rhs = jnp.sum(recv_ref[...].astype(f32), axis=0)
    rhs_ref[...] = rhs
    low_ref[...] = rhs.astype(bf16)
    coef_ref[...] = coefs_of(rhs, basis_ref)


def near_kernel(pick_ref, blocks_ref, low_ref, other_ref, out_ref):
    clusters, width = out_ref.shape
    other = other_ref[...].astype(f32)
    for t in range(clusters):
        low = low_ref[t : t + 1, :]
        chosen = other[0:1, :]
        for n in range(1, other.shape[0]):
            chosen = jnp.where(pick_ref[t] == n, other[n : n + 1, :], chosen)
        out_ref[t : t + 1, :] = dot_nt(low, blocks_ref[t, 0]) + dot_nt(
            chosen.astype(bf16), blocks_ref[t, 1]
        )


def far_of(index_ref, table_ref, couple_ref, target_ref, t):
    blocks = couple_ref.shape[1]
    total = None
    for b in range(blocks):
        row = table_ref[pl.ds(index_ref[t * blocks + b], 1), :]
        part = couple_ref[t, b] * row
        total = part if total is None else total + part
    mixed = jnp.sum(total, axis=1, keepdims=True)
    return jnp.sum(mixed * target_ref[t], axis=0, keepdims=True)


def step_kernel(
    index_ref, table_ref, couple_ref, target_ref, rhs_ref, near_ref, basis_ref, *out_refs
):
    clusters = rhs_ref.shape[0]
    far = jnp.concatenate(
        [far_of(index_ref, table_ref, couple_ref, target_ref, t) for t in range(clusters)], axis=0
    )
    density = rhs_ref[...] - near_ref[...] - far
    out_refs[0][...] = density
    if len(out_refs) > 1:
        out_refs[1][...] = density.astype(bf16)
        out_refs[2][...] = coefs_of(density, basis_ref)


def start(received, basis):
    clusters, rank, width = basis.shape
    return pl.pallas_call(
        start_kernel,
        out_shape=(
            jax.ShapeDtypeStruct((clusters, width), f32),
            jax.ShapeDtypeStruct((clusters, width), bf16),
            jax.ShapeDtypeStruct((1, LANES), f32),
        ),
        in_specs=[VMEM] * 2,
        out_specs=(VMEM,) * 3,
        cost_estimate=pl.CostEstimate(flops=500_000, bytes_accessed=400_000, transcendentals=0),
        name="start",
    )(received, basis)


def near_part(pick, blocks, low, other):
    return pl.pallas_call(
        near_kernel,
        out_shape=jax.ShapeDtypeStruct(low.shape, f32),
        in_specs=[SMEM, VMEM, VMEM, VMEM],
        out_specs=VMEM,
        cost_estimate=pl.CostEstimate(flops=2_000_000, bytes_accessed=1_200_000, transcendentals=0),
        name="near_part",
    )(pick, blocks, low, other)


def step(index, table, couple, target, rhs, near, basis, last):
    clusters, rank, width = basis.shape
    shapes = [jax.ShapeDtypeStruct((clusters, width), f32)]
    if not last:
        shapes.append(jax.ShapeDtypeStruct((clusters, width), bf16))
        shapes.append(jax.ShapeDtypeStruct((1, LANES), f32))
    return pl.pallas_call(
        step_kernel,
        out_shape=tuple(shapes),
        in_specs=[SMEM] + [VMEM] * 6,
        out_specs=(VMEM,) * len(shapes),
        cost_estimate=pl.CostEstimate(flops=500_000, bytes_accessed=500_000, transcendentals=0),
        name="step",
    )(index, table, couple, target, rhs, near, basis)


def local(
    shape_coef,
    force_coef,
    near_cell,
    near_dest,
    near_slot,
    panel_centers,
    near_blocks,
    near_pick,
    src_basis,
    far_couple,
    far_src,
    far_rank,
    tgt_basis,
    cluster_slot,
):
    walls = lax.axis_size(WALL)
    clusters, width = panel_centers.shape
    rank = far_couple.shape[2]
    harmonic = harmonics(ORDER)
    quads = harmonic.shape[0]
    padded = -(-quads // LANES) * LANES
    grid = np.zeros((harmonic.shape[1], padded), np.float32)
    grid[:, :quads] = harmonic.T
    grid = jnp.asarray(grid, f32).astype(bf16)
    harmonic = jnp.asarray(harmonic, f32).astype(bf16)

    centers = gather_wall(panel_centers)
    sources = near_sources(near_cell, shape_coef, force_coef, grid)
    surface = jnp.einsum(
        "qs,asc->aqc", harmonic, shape_coef, preferred_element_type=jnp.float32
    ).astype(bf16)

    source_rows = jnp.take(cluster_slot, far_src.reshape(-1), axis=0)
    per_row = LANES // rank
    index, offset = table_place(source_rows, clusters, rank)
    levels = jnp.arange(rank, dtype=jnp.int32)
    keep = (levels[None, None, :, None] < far_rank[:, :, None, None]) & (
        levels[None, None, None, :] < far_rank[:, :, None, None]
    )
    masked = jnp.where(keep, far_couple, jnp.zeros_like(far_couple))
    lane_part = jnp.arange(LANES, dtype=jnp.int32) // rank
    here = lane_part[None, None, None, :] == offset.reshape(far_src.shape)[:, :, None, None]
    couple = jnp.where(here, jnp.tile(masked, (1, 1, 1, per_row)), 0.0)
    basis = jnp.swapaxes(src_basis, 1, 2)

    target = near_slot * walls + near_dest
    sums = pair_sums(target, sources, centers, walls)
    received = exchange_wall(sums, clusters)
    rhs, low, coef = start(received, basis)
    for k in range(ITERS):
        other = shifted(low, WALL, 1)
        near = near_part(near_pick, near_blocks, low, other)
        table = gather_all(coef, clusters, rank)
        out = step(index, table, couple, tgt_basis, rhs, near, basis, k == ITERS - 1)
        if k < ITERS - 1:
            density, low, coef = out
        else:
            (density,) = out
    return (surface, density)


def gather_wall(panel_centers):
    walls = lax.axis_size(WALL)
    flat = panel_centers.reshape(1, 1, -1)
    pieces = jnp.broadcast_to(flat, (walls, 1, flat.shape[2]))
    pieces = lax.all_to_all(pieces, WALL, split_axis=0, concat_axis=0, tiled=True)
    return pieces.reshape(-1, LANES)


def exchange_wall(sums, clusters):
    walls = sums.shape[0]
    pieces = sums.astype(bf16).reshape(walls, clusters, -1)
    return lax.all_to_all(pieces, WALL, split_axis=0, concat_axis=0, tiled=True)


def gather_all(coef, clusters, rank):
    walls = lax.axis_size(WALL)
    cells = lax.axis_size(CELLS)
    groups = LANES // (clusters * rank)
    lane = jnp.arange(LANES, dtype=jnp.int32) // (clusters * rank)
    mine = jnp.where(lane[None, :] == lax.axis_index(WALL) // (walls // groups), coef, 0.0)
    pieces = jnp.broadcast_to(mine[:, None, :], (walls, 1, LANES))
    pieces = lax.all_to_all(pieces, WALL, split_axis=0, concat_axis=0, tiled=True)
    group = jnp.sum(pieces.reshape(groups, walls // groups, LANES), axis=0)
    pieces = jnp.broadcast_to(group.reshape(1, 1, -1), (cells, 1, group.size))
    pieces = lax.all_to_all(pieces, CELLS, split_axis=0, concat_axis=0, tiled=True)
    return pieces.reshape(-1, LANES)


def table_place(slots, clusters, rank):
    walls = lax.axis_size(WALL)
    groups = LANES // (clusters * rank)
    lines = walls // groups
    device = slots // clusters
    cell, wall = device // walls, device % walls
    return cell * lines + wall % lines, wall // lines * clusters + slots % clusters


def solution(mesh):
    finer = Mesh(mesh.devices.reshape(4, 4, 32, 2), ("cells_0", "cells_1", "wall_0", "wall_1"))
    return jax.shard_map(
        local,
        mesh=finer,
        in_specs=(
            P(None, None, CELLS_WALL),
            P(None, None, CELLS_WALL),
            P(CELLS_WALL),
            P(CELLS_WALL),
            P(CELLS_WALL),
            P(CELLS_WALL, None),
            P(CELLS_WALL, None, None, None),
            P(CELLS_WALL),
            P(CELLS_WALL, None, None),
            P(CELLS_WALL, None, None, None),
            P(CELLS_WALL, None),
            P(CELLS_WALL, None),
            P(CELLS_WALL, None, None),
            P(),
        ),
        out_specs=(P(None, None, CELLS_WALL), P(CELLS_WALL, None)),
        check_vma=False,
    )
```

time: 455 us -> 221 us (0.49)
  blocking collectives: 152 us -> 0 us
  other arithmetic: 94.2 us -> 4.96 us
  Pallas kernels: 0 us -> 36.1 us
  local copies, waits for them, and re-layouts: 43.3 us -> 12.7 us
  starting transfers between devices: 52.3 us -> 62.7 us
    all_gather x8 -> x0, blocking collectives: 152 us -> none  [gather_in_order(): pieces = lax.all_gather(pieces, axes[k])]
    reduce_sum x17 -> x2, other arithmetic: 74.4 us -> 0.01 us  [gather_all(): group = jnp.sum(pieces.reshape(groups, walls // groups, LANES), axis=0)]
    pallas_call x0 -> x7, Pallas kernels: none -> 36.1 us  [the longest x1 22.4 us: pair_sums(): pl.pallas_call(pairs_kernel, out_shape=jax.ShapeDtypeStruct((walls, width...]
    all_to_all x2 -> x6, starting transfers between devices: 44.8 us -> 59.4 us  [the longest x1 30.4 us: gather_wall(): lax.all_to_all(pieces, WALL, split_axis=0, concat_axis=0, tiled=True)]
    reshape x19 -> x5, local copies, waits for them, and re-layouts: 13.9 us -> 3.57 us  [the longest x1 1.36 us: near_sources(): near_cell.reshape(rows, 1)]
    dynamic_update_slice x16 -> x0, other arithmetic: 9.69 us -> none  [stokes_rows(): lax.map(kernel_block, (points.reshape(groups, width, 3, points.shape[2]),...]
    dynamic_slice x48 -> x0, local copies, waits for them, and re-layouts: 8.19 us -> none  [stokes_rows(): lax.map(kernel_block, (points.reshape(groups, width, 3, points.shape[2]),...]
    gather x9 -> x2, local copies, waits for them, and re-layouts: 5.65 us -> 0.74 us  [local(): source_rows = jnp.take(cluster_slot, far_src.reshape(-1), axis=0)]
  transfers between devices with their start and end apart: 4 -> 8, of which waited for: 2 -> 6; matrix products, arithmetic and copies ran while one was open for 5% -> 4% of each run, Pallas kernels for 0% -> 4%
where the time goes in v1:
time: 221 us; the launch traced here: 220 us
  waiting for transfers between devices  101 us (46%)
  starting transfers between devices  62.7 us (28%)
  Pallas kernels  36.1 us (16%)
  local copies, waits for them, and re-layouts  12.7 us (6%)
  other arithmetic  4.96 us (2%)
    all_to_all x2, waiting for transfers between devices, gather_all(): lax.all_to_all(pieces, WALL, split_axis=0, concat_axis=0, tiled=True)  40.2 us
    all_to_all x1, starting transfers between devices, gather_wall(): lax.all_to_all(pieces, WALL, split_axis=0, concat_axis=0, tiled=True)  30.4 us
    all_to_all x1, waiting for transfers between devices, gather_wall(): lax.all_to_all(pieces, WALL, split_axis=0, concat_axis=0, tiled=True)  28 us
    all_to_all x1, waiting for transfers between devices, exchange_wall(): return lax.all_to_all(pieces, WALL, split_axis=0, concat_axis=0, tiled=True)  27.7 us
    pallas_call x1, Pallas kernels, pair_sums(): pl.pallas_call(pairs_kernel, out_shape=jax.ShapeDtypeStruct((walls, width...  22.4 us
    all_to_all x2, starting transfers between devices, gather_all(): lax.all_to_all(pieces, WALL, split_axis=0, concat_axis=0, tiled=True)  12.9 us
    all_to_all x2, starting transfers between devices, gather_all(): lax.all_to_all(pieces, CELLS, split_axis=0, concat_axis=0, tiled=True)  10.4 us
    all_to_all x1, starting transfers between devices, exchange_wall(): return lax.all_to_all(pieces, WALL, split_axis=0, concat_axis=0, tiled=True)  5.68 us
  transfers between devices with their start and end apart: 8, of which 6 were waited for; matrix products, arithmetic and copies ran while one was open for 4% of the time, Pallas kernels for 4%

profile of v1, /device:TPU:1, one launch (start us, length us, event | category | flops | bytes accessed | tf_op | source)
XLA Modules:
  0.0 220.3 jit_solution(651471949085558704)
XLA Ops:
  0.6 0.7 broadcast_in_dim.66
  1.3 0.8 broadcast_in_dim.67
  2.1 30.4 %all-to-all-start = ((f32[64,1,768]{2,1,0:T(1,128)}), f32[64,1,768]{2,1,0:T(1,128)S(1)}, u32[]{:S(2)}, u32[]{:S(2)}) async-start(f32[64,1,768]{2,1,0:T(1,128)} %broadcast_in_dim.67), calls=%async_computation | async-start | bytes 393216 | tf_op jit(solution)/shard_map/all_to_all | solution.py:395
  32.5 1.2 fusion.8
  33.7 0.7 copy.27.tcol_ref
  34.4 1.4 copy.26.cell_ref
  35.8 0.8 reshape.232
  37.3 3.7 %near_sources.1.src_ref = bf16[6,64,640]{2,1,0:T(8,128)(2,1)} custom-call(s32[64,1]{1,0:T(8,128)} %copy.26.cell_ref, bf16[3,289,256]{2,1,0:T(8,128)(2,1)} %shape_ref.1, bf16[3,289,256]{2,1,0:T(8,128)(2,1)} %force_ref.1, bf16[289,640]{1,0:T(8,128)(2,1)} %constant.154.grid_ref), custom_call_target="tpu_custom_call" | custom-call | flops 200000000 | bytes 2500000 | tf_op jit(solution)/shard_map/near_sources/pallas_call | solution.py:97
  41.0 28.0 %all-to-all-done = f32[64,1,768]{2,1,0:T(1,128)S(1)} async-done(((f32[64,1,768]{2,1,0:T(1,128)}), f32[64,1,768]{2,1,0:T(1,128)S(1)}, u32[]{:S(2)}, u32[]{:S(2)}) %all-to-all-start) | async-done | bytes 196640 | tf_op jit(solution)/shard_map/all_to_all | solution.py:395
  69.0 0.7 copy-done.5
  69.7 22.4 %pair_sums.1 = f32[64,768]{1,0:T(8,128)} custom-call(s32[64,1]{1,0:T(8,128)} %copy.27.tcol_ref, s32[1,64]{1,0:T(1,128)} %get-tuple-element.12.trow_ref, bf16[6,64,640]{2,1,0:T(8,128)(2,1)} %near_sources.1.src_ref, f32[384,128]{1,0:T(8,128)} %bitcast.35), custom_call_target="tpu_custom_call" | custom-call | flops 1000000000 | bytes 1000000 | tf_op jit(solution)/shard_map/pair_sums/pallas_call | solution.py:207
  92.1 0.9 convert_element_type.19
  93.7 5.7 %all-to-all-start.1 = ((bf16[64,2,384]{2,1,0:T(2,128)(2,1)}), bf16[64,2,384]{2,1,0:T(2,128)(2,1)S(1)}, u32[]{:S(2)}, u32[]{:S(2)}) async-start(bf16[64,2,384]{2,1,0:T(2,128)(2,1)} %reshape.237), calls=%async_computation.1 | async-start | bytes 196608 | tf_op jit(solution)/shard_map/all_to_all | solution.py:402
  99.7 27.7 %all-to-all-done.1.recv_ref = bf16[64,2,384]{2,1,0:T(2,128)(2,1)S(1)} async-done(((bf16[64,2,384]{2,1,0:T(2,128)(2,1)}), bf16[64,2,384]{2,1,0:T(2,128)(2,1)S(1)}, u32[]{:S(2)}, u32[]{:S(2)}) %all-to-all-start.1) | async-done | bytes 98336 | tf_op jit(solution)/shard_map/all_to_all | solution.py:402
  128.0 1.8 start.1
  131.1 5.8 %all-to-all-start.2 = ((f32[64,1,128]{2,1,0:T(1,128)}), f32[64,1,128]{2,1,0:T(1,128)S(1)}, u32[]{:S(2)}, u32[]{:S(2)}) async-start(f32[64,1,128]{2,1,0:T(1,128)} %broadcast_in_dim.70), calls=%async_computation.2 | async-start | bytes 65536 | tf_op jit(solution)/shard_map/all_to_all | solution.py:412
  138.2 1.6 collective-permute-start
  139.8 19.5 %all-to-all-done.2 = f32[64,1,128]{2,1,0:T(1,128)S(1)} async-done(((f32[64,1,128]{2,1,0:T(1,128)}), f32[64,1,128]{2,1,0:T(1,128)S(1)}, u32[]{:S(2)}, u32[]{:S(2)}) %all-to-all-start.2) | async-done | bytes 32800 | tf_op jit(solution)/shard_map/all_to_all | solution.py:412
  159.3 0.7 broadcast_in_dim.72
  160.0 6.9 %all-to-all-start.3 = ((f32[16,1,2048]{2,1,0:T(1,128)}), f32[16,1,2048]{2,1,0:T(1,128)S(1)}, u32[]{:S(2)}, u32[]{:S(2)}) async-start(f32[16,1,2048]{2,1,0:T(1,128)} %broadcast_in_dim.72), calls=%async_computation.3 | async-start | bytes 262144 | tf_op jit(solution)/shard_map/all_to_all | solution.py:415
  168.1 2.3 %near_part.2.near_ref = f32[2,384]{1,0:T(2,128)} custom-call(s32[2]{0:T(128)} %pick_ref.3, bf16[2,2,384,384]{3,2,1,0:T(8,128)(2,1)} %blocks_ref.3, bf16[2,384]{1,0:T(2,128)(2,1)} %get-tuple-element.9.low_ref, bf16[2,384]{1,0:T(2,128)(2,1)} %copy-done.8), custom_call_target="tpu_custom_call" | custom-call | flops 2000000 | bytes 1200000 | tf_op jit(solution)/shard_map/near_part/pallas_call | solution.py:303
  170.4 3.3 %all-to-all-done.3 = f32[16,1,2048]{2,1,0:T(1,128)S(1)} async-done(((f32[16,1,2048]{2,1,0:T(1,128)}), f32[16,1,2048]{2,1,0:T(1,128)S(1)}, u32[]{:S(2)}, u32[]{:S(2)}) %all-to-all-start.3) | async-done | bytes 131104 | tf_op jit(solution)/shard_map/all_to_all | solution.py:415
  174.3 1.9 step.2
  177.5 7.1 %all-to-all-start.4 = ((f32[64,1,128]{2,1,0:T(1,128)}), f32[64,1,128]{2,1,0:T(1,128)S(1)}, u32[]{:S(2)}, u32[]{:S(2)}) async-start(f32[64,1,128]{2,1,0:T(1,128)} %broadcast_in_dim.77), calls=%async_computation.4 | async-start | bytes 65536 | tf_op jit(solution)/shard_map/all_to_all | solution.py:412
  184.6 1.7 collective-permute-start.1
  186.2 20.7 %all-to-all-done.4 = f32[64,1,128]{2,1,0:T(1,128)S(1)} async-done(((f32[64,1,128]{2,1,0:T(1,128)}), f32[64,1,128]{2,1,0:T(1,128)S(1)}, u32[]{:S(2)}, u32[]{:S(2)}) %all-to-all-start.4) | async-done | bytes 32800 | tf_op jit(solution)/shard_map/all_to_all | solution.py:412
  207.0 0.7 broadcast_in_dim.79
  207.7 3.5 %all-to-all-start.5 = ((f32[16,1,2048]{2,1,0:T(1,128)}), f32[16,1,2048]{2,1,0:T(1,128)S(1)}, u32[]{:S(2)}, u32[]{:S(2)}) async-start(f32[16,1,2048]{2,1,0:T(1,128)} %broadcast_in_dim.79), calls=%async_computation.5 | async-start | bytes 262144 | tf_op jit(solution)/shard_map/all_to_all | solution.py:415
  211.2 1.6 fusion
  213.4 2.3 %near_part.3.near_ref = f32[2,384]{1,0:T(2,128)} custom-call(s32[2]{0:T(128)} %pick_ref.3, bf16[2,2,384,384]{3,2,1,0:T(8,128)(2,1)} %blocks_ref.3, bf16[2,384]{1,0:T(2,128)(2,1)} %get-tuple-element.11.low_ref, bf16[2,384]{1,0:T(2,128)(2,1)} %copy-done.9), custom_call_target="tpu_custom_call" | custom-call | flops 2000000 | bytes 1200000 | tf_op jit(solution)/shard_map/near_part/pallas_call | solution.py:303
  215.7 2.3 %all-to-all-done.5 = f32[16,1,2048]{2,1,0:T(1,128)S(1)} async-done(((f32[16,1,2048]{2,1,0:T(1,128)}), f32[16,1,2048]{2,1,0:T(1,128)S(1)}, u32[]{:S(2)}, u32[]{:S(2)}) %all-to-all-start.5) | async-done | bytes 131104 | tf_op jit(solution)/shard_map/all_to_all | solution.py:415
  218.6 1.7 step.3
  (48 shorter events, 9.1 us)
Async XLA Ops:
  0.6 35.9 %copy-start = (s32[2048]{0:T(1024)S(1)}, s32[2048]{0:T(1024)}, u32[]{:S(2)}) copy-start(s32[2048]{0:T(1024)} %param.29) | copy-start | bytes 24580
  2.1 66.9 %all-to-all-start = ((f32[64,1,768]{2,1,0:T(1,128)}), f32[64,1,768]{2,1,0:T(1,128)S(1)}, u32[]{:S(2)}, u32[]{:S(2)}) async-start(f32[64,1,768]{2,1,0:T(1,128)} %broadcast_in_dim.67), calls=%async_computation | async-start | bytes 393216 | tf_op jit(solution)/shard_map/all_to_all | solution.py:395
  69.0 0.7 copy-start.5
  69.7 29.7 %copy-start.11 = (s32[2,8]{1,0:T(2,128)S(1)}, s32[2,8]{1,0:T(2,128)}, u32[]{:S(2)}) copy-start(s32[2,8]{1,0:T(2,128)} %param.26) | copy-start | bytes 196
  69.7 29.8 %copy-start.10 = (s32[2,8]{1,0:T(2,128)S(1)}, s32[2,8]{1,0:T(2,128)}, u32[]{:S(2)}) copy-start(s32[2,8]{1,0:T(2,128)} %param.27) | copy-start | bytes 196
  69.7 29.9 %copy-start.6 = (f32[2,8,16,16]{3,2,1,0:T(8,128)S(1)}, f32[2,8,16,16]{3,2,1,0:T(8,128)}, u32[]{:S(2)}) copy-start(f32[2,8,16,16]{3,2,1,0:T(8,128)} %param.25) | copy-start | bytes 49156
  93.7 33.6 %all-to-all-start.1 = ((bf16[64,2,384]{2,1,0:T(2,128)(2,1)}), bf16[64,2,384]{2,1,0:T(2,128)(2,1)S(1)}, u32[]{:S(2)}, u32[]{:S(2)}) async-start(bf16[64,2,384]{2,1,0:T(2,128)(2,1)} %reshape.237), calls=%async_computation.1 | async-start | bytes 196608 | tf_op jit(solution)/shard_map/all_to_all | solution.py:402
  127.4 0.6 copy-start.4
  131.1 28.2 %all-to-all-start.2 = ((f32[64,1,128]{2,1,0:T(1,128)}), f32[64,1,128]{2,1,0:T(1,128)S(1)}, u32[]{:S(2)}, u32[]{:S(2)}) async-start(f32[64,1,128]{2,1,0:T(1,128)} %broadcast_in_dim.70), calls=%async_computation.2 | async-start | bytes 65536 | tf_op jit(solution)/shard_map/all_to_all | solution.py:412
  137.1 1.1 copy-start.7
  138.2 29.3 %collective-permute-start = (bf16[2,384]{1,0:T(2,128)(2,1)S(1)}, bf16[2,384]{1,0:T(2,128)(2,1)S(1)}, u32[]{:S(2)}, u32[]{:S(2)}) collective-permute-start(bf16[2,384]{1,0:T(2,128)(2,1)S(1)} %copy-done.7), channel_id=1, source_target_pairs={{0,1},{1,2},{2,3},{3,4},{4,5},{5,6},{6,7},{7,8},{8,9},{9,10},{10,1... | collective-permute-start | bytes 4616 | tf_op jit(solution)/shard_map/ppermute | solution.py:31
  160.0 51.2 %copy-start.3 = (bf16[3,289,256]{2,1,0:T(8,128)(2,1)S(1)}, bf16[3,289,256]{2,1,0:T(8,128)(2,1)}, u32[]{:S(2)}) copy-start(bf16[3,289,256]{2,1,0:T(8,128)(2,1)} %shape_ref.1) | copy-start | bytes 1331716
  160.0 51.2 %copy-start.12 = (bf16[578,289,1]{0,1,2:T(8,128)(2,1)S(1)}, bf16[578,289,1]{0,1,2:T(8,128)(2,1)}, u32[]{:S(2)}) copy-start(bf16[578,289,1]{0,1,2:T(8,128)(2,1)} %constant.155) | copy-start | bytes 1002256
  160.0 13.6 %all-to-all-start.3 = ((f32[16,1,2048]{2,1,0:T(1,128)}), f32[16,1,2048]{2,1,0:T(1,128)S(1)}, u32[]{:S(2)}, u32[]{:S(2)}) async-start(f32[16,1,2048]{2,1,0:T(1,128)} %broadcast_in_dim.72), calls=%async_computation.3 | async-start | bytes 262144 | tf_op jit(solution)/shard_map/all_to_all | solution.py:415
  167.5 0.6 copy-start.8
  173.7 0.7 copy-start.1
  177.5 29.5 %all-to-all-start.4 = ((f32[64,1,128]{2,1,0:T(1,128)}), f32[64,1,128]{2,1,0:T(1,128)S(1)}, u32[]{:S(2)}, u32[]{:S(2)}) async-start(f32[64,1,128]{2,1,0:T(1,128)} %broadcast_in_dim.77), calls=%async_computation.4 | async-start | bytes 65536 | tf_op jit(solution)/shard_map/all_to_all | solution.py:412
  184.6 28.2 %collective-permute-start.1 = (bf16[2,384]{1,0:T(2,128)(2,1)}, bf16[2,384]{1,0:T(2,128)(2,1)S(1)}, u32[]{:S(2)}, u32[]{:S(2)}) collective-permute-start(bf16[2,384]{1,0:T(2,128)(2,1)} %get-tuple-element.11.low_ref), channel_id=1, source_target_pairs={{0,1},{1,2},{2,3},{3,4},{4,5},{5,6},{6,7},{7,8},{8,9},{9,10},{10,1... | collective-permute-start | bytes 4616 | tf_op jit(solution)/shard_map/ppermute | solution.py:31
  207.7 10.2 %all-to-all-start.5 = ((f32[16,1,2048]{2,1,0:T(1,128)}), f32[16,1,2048]{2,1,0:T(1,128)S(1)}, u32[]{:S(2)}, u32[]{:S(2)}) async-start(f32[16,1,2048]{2,1,0:T(1,128)} %broadcast_in_dim.79), calls=%async_computation.5 | async-start | bytes 262144 | tf_op jit(solution)/shard_map/all_to_all | solution.py:415
  212.8 0.6 copy-start.9
  217.9 0.7 copy-start.2

commit v2 on v1

--- a/solution.py
+++ b/solution.py
@@ -13,13 +13,18 @@
 ORDER = 16
 ITERS = 2
 WALL = ("wall_0", "wall_1")
-CELLS = ("cells_0", "cells_1")
+CHIPS = "wall_0"
+CORE = "wall_1"
+PLANE = ("cells_0", "cells_1", "wall_1")
 CELLS_WALL = ("cells_0", "cells_1", "wall_0", "wall_1")
 
 soft_core = 0.25
 stokes_scale = 1.0 / (8.0 * math.pi)
 LANES = 128
+REACH = 2.0
+FIXED = 32767.0
 PANELS = 128
+OWN = 2
 f32 = jnp.float32
 bf16 = jnp.bfloat16
 VMEM = pl.BlockSpec(memory_space=pltpu.VMEM)
@@ -63,6 +68,14 @@
     return np.stack(columns, axis=1)
 
 
+def kept(shape, dtype):
+    return pltpu.VMEM(shape, dtype)
+
+
+def held(*arrays):
+    return [pltpu.with_memory_space_constraint(array, pltpu.VMEM) for array in arrays]
+
+
 def dot_nn(a, b):
     return lax.dot_general(a, b, (((1,), (0,)), ((), ())), preferred_element_type=f32)
 
@@ -85,7 +98,8 @@
 def sources_kernel(cell_ref, shape_ref, force_ref, grid_ref, out_ref):
     rows = out_ref.shape[1]
     cells = shape_ref.shape[2]
-    pick = (lax.broadcasted_iota(jnp.int32, (rows, cells), 1) == cell_ref[...]).astype(bf16)
+    pick = (lax.broadcasted_iota(jnp.int32, (cells, rows), 0) == cell_ref[...]).astype(f32)
+    pick = jnp.transpose(pick).astype(bf16)
     for base, ref in ((0, shape_ref), (3, force_ref)):
         for a in range(3):
             coefs = dot_nt(pick, ref[a]).astype(bf16)
@@ -96,12 +110,12 @@
     rows = near_cell.shape[0]
     return pl.pallas_call(
         sources_kernel,
-        out_shape=jax.ShapeDtypeStruct((6, rows, grid.shape[1]), bf16),
+        out_shape=kept((6, rows, grid.shape[1]), bf16),
         in_specs=[VMEM] * 4,
         out_specs=VMEM,
         cost_estimate=pl.CostEstimate(flops=200_000_000, bytes_accessed=2_500_000, transcendentals=0),
         name="near_sources",
-    )(near_cell.reshape(rows, 1), shape_coef, force_coef, grid)
+    )(near_cell.reshape(1, rows), shape_coef, force_coef, grid)
 
 
 def put(ref, k, value):
@@ -116,13 +130,21 @@
     )
 
 
-def pairs_kernel(tcol_ref, trow_ref, src_ref, ctr_ref, out_ref, ysc, gsc, bsc, mom, xsc):
+def pairs_kernel(
+    cores, dest_ref, slot_ref, src_ref, ctr_ref, out_ref, ysc, gsc, bsc, mom, xsc, csc, *bufs
+):
     rows, quads = src_ref.shape[1], src_ref.shape[2]
-    walls, width = out_ref.shape
+    lines = OWN * 3
+    walls = out_ref.shape[0] // lines
+    third = len(bufs) // 3
+    rho_bufs, inv_bufs, cube_bufs = bufs[:third], bufs[third : 2 * third], bufs[2 * third :]
     pan = PANELS
-    own = width // (3 * pan)
+    own = OWN
     clusters = walls * own
-    lines = width // LANES
+    dest, slot = dest_ref[...], slot_ref[...]
+    chips = walls // cores
+    place = slot * walls + lax.rem(dest, cores) * chips + lax.div(dest, cores)
+    target = slot * walls + dest
     y = [src_ref[a].astype(f32) for a in range(3)]
     f = [src_ref[3 + a].astype(f32) for a in range(3)]
     y2 = y[0] * y[0] + y[1] * y[1] + y[2] * y[2]
@@ -141,12 +163,14 @@
         for b in range(3):
             put(gsc, 4 + 3 * a + b, y[a] * f[b])
         put(gsc, 13 + a, y[a] * yf)
-    pick = (lax.broadcasted_iota(jnp.int32, (rows, clusters), 1) == tcol_ref[...]).astype(bf16)
+    csc[...] = ctr_ref[...].astype(jnp.int32).astype(f32) * (REACH / FIXED)
+    pick = (lax.broadcasted_iota(jnp.int32, (clusters, rows), 0) == place).astype(f32)
+    pick = jnp.transpose(pick).astype(bf16)
     x = []
     for a in range(3):
         total = None
         spots = jnp.concatenate(
-            [ctr_ref[pl.ds(3 * t + a, walls, stride=lines), :] for t in range(own)], axis=0
+            [csc[pl.ds(own * a + t, walls, stride=lines), :] for t in range(own)], axis=0
         )
         for i, piece in enumerate(split3(spots)):
             part = dot_nn(pick, piece.astype(bf16))
@@ -161,30 +185,41 @@
         bsc[pl.ds((12 + k) * rows, rows), :] = piece
     bsc[pl.ds(15 * rows, rows), :] = jnp.zeros((rows, pan), f32)
 
-    def row(r, carry):
-        yr = get(ysc, r, rows).astype(bf16)
-        br = bsc[pl.ds(r, 16, stride=rows), :]
-        g = get(gsc, r, rows)
-        g_hi = g.astype(bf16)
-        g_lo = (g - g_hi.astype(f32)).astype(bf16)
-        rho2 = dot_tn(yr, br.astype(bf16))
-        inverse = lax.rsqrt(rho2)
-        cube = inverse * inverse * inverse
-        c_hi = cube.astype(bf16)
-        c_lo = (cube - c_hi.astype(f32)).astype(bf16)
-        i_hi = inverse.astype(bf16)
-        i_lo = (inverse - i_hi.astype(f32)).astype(bf16)
-        first = dot_nn(jnp.concatenate([g_hi, g_lo], axis=0), c_hi)
-        mom[pl.ds(r, 16, stride=rows), :] = first[:16] + first[16:] + dot_nn(g_hi, c_lo)
-        plain = dot_nn(g_hi, i_hi) + dot_nn(g_hi, i_lo)
-        mom[pl.ds(16 * rows + r, 8, stride=rows), :] = plain[:8]
+    lanes = len(rho_bufs) // 2
+
+    def turn(i, old, new):
+        held_inv, held_cube = inv_bufs[old::2], cube_bufs[old::2]
+        next_inv, next_cube = inv_bufs[new::2], cube_bufs[new::2]
+        held_rho, next_rho = rho_bufs[old::2], rho_bufs[new::2]
+        for n in range(lanes):
+            r = jnp.clip(lanes * (i - 2) + n, n, rows - lanes + n)
+            g = get(gsc, r, rows)
+            g_hi = g.astype(bf16)
+            g_lo = (g - g_hi.astype(f32)).astype(bf16)
+            first = dot_nt(jnp.concatenate([g_hi, g_lo], axis=0), held_cube[n][...])
+            plain = dot_nt(g_hi, held_inv[n][...])
+            mom[pl.ds(r, 16, stride=rows), :] = first[:16] + first[16:]
+            mom[pl.ds(16 * rows + r, 8, stride=rows), :] = plain[:8]
+        for n in range(lanes):
+            inverse = lax.rsqrt(held_rho[n][...])
+            next_inv[n][...] = inverse.astype(bf16)
+            next_cube[n][...] = (inverse * inverse * inverse).astype(bf16)
+        for n in range(lanes):
+            r = jnp.minimum(lanes * i + n, rows - lanes + n)
+            yr = get(ysc, r, rows).astype(bf16)
+            br = bsc[pl.ds(r, 16, stride=rows), :].astype(bf16)
+            next_rho[n][...] = dot_tn(br, yr)
+
+    def turns(i, carry):
+        turn(2 * i, 0, 1)
+        turn(2 * i + 1, 1, 0)
         return carry
 
-    lax.fori_loop(0, rows, row, 0, unroll=PAIR_UNROLL)
+    lax.fori_loop(0, (rows // lanes + 2 + 1) // 2, turns, 0, unroll=TURN_UNROLL)
     x = [xsc[pl.ds(a * rows, rows), :] for a in range(3)]
     moment = [mom[pl.ds(c * rows, rows), :] for c in range(19)]
     common = x[0] * moment[0] + x[1] * moment[1] + x[2] * moment[2] - moment[3]
-    drop = (lax.broadcasted_iota(jnp.int32, (clusters, rows), 0) == trow_ref[...]).astype(bf16)
+    drop = (lax.broadcasted_iota(jnp.int32, (clusters, rows), 0) == target).astype(bf16)
     for a in range(3):
         local_part = x[0] * moment[4 + 3 * a] + x[1] * moment[5 + 3 * a] + x[2] * moment[6 + 3 * a]
         velocity = moment[16 + a] + x[a] * common - (local_part - moment[13 + a])
@@ -194,19 +229,21 @@
             part = dot_nn(drop, piece.astype(bf16))
             total = part if total is None else total + part
         for t in range(own):
-            out_ref[:, pl.ds((3 * t + a) * pan, pan)] = total[t * walls : (t + 1) * walls, :]
-
-
-PAIR_UNROLL = 8
-
-
-def pair_sums(target, sources, centers, walls):
+            part = total[t * walls : (t + 1) * walls, :]
+            csc[pl.ds(own * a + t, walls, stride=lines), :] = part
+    out_ref[...] = csc[...].astype(out_ref.dtype)
+
+
+PAIR_LANES = 4
+TURN_UNROLL = 1
+
+
+def pair_sums(dest, slot, sources, centers, live, cores):
     rows, quads = sources.shape[1:]
-    width = centers.shape[0] * LANES // walls
     pan = PANELS
     return pl.pallas_call(
-        pairs_kernel,
-        out_shape=jax.ShapeDtypeStruct((walls, width), f32),
+        functools.partial(pairs_kernel, cores),
+        out_shape=jax.ShapeDtypeStruct(centers.shape, bf16),
         in_specs=[VMEM] * 4,
         out_specs=VMEM,
         scratch_shapes=[
@@ -215,12 +252,15 @@
             pltpu.VMEM((16 * rows, pan), f32),
             pltpu.VMEM((24 * rows, pan), f32),
             pltpu.VMEM((3 * rows, pan), f32),
-        ],
+            pltpu.VMEM(centers.shape, f32),
+        ]
+        + [pltpu.VMEM((pan, quads), f32)] * (2 * PAIR_LANES)
+        + [pltpu.VMEM((pan, quads), bf16)] * (4 * PAIR_LANES),
         cost_estimate=pl.CostEstimate(
             flops=1_000_000_000, bytes_accessed=1_000_000, transcendentals=5_000_000
         ),
         name="pair_sums",
-    )(target.reshape(rows, 1), target.reshape(1, rows), sources, centers)
+    )(*held(dest.reshape(1, rows), slot.reshape(1, rows), sources, centers))
 
 
 def coefs_of(density, basis_ref):
@@ -238,11 +278,30 @@
     return jnp.concatenate(parts * (LANES // (len(parts) * parts[0].shape[1])), axis=1)
 
 
-def start_kernel(recv_ref, basis_ref, rhs_ref, low_ref, coef_ref):
-    rhs = jnp.sum(recv_ref[...].astype(f32), axis=0)
+def send_coefs(group_ref, density, basis_ref, coef_ref):
+    clusters, rank, _ = basis_ref.shape
+    lane = lax.broadcasted_iota(jnp.int32, (1, LANES), 1) // (clusters * rank)
+    mine = jnp.where(lane == group_ref[0], coefs_of(density, basis_ref), 0.0)
+    coef_ref[...] = jnp.broadcast_to(mine, coef_ref.shape)
+
+
+def start_kernel(group_ref, recv_ref, basis_ref, rhs_ref, low_ref, coef_ref):
+    own, width = rhs_ref.shape
+    lines = own * width // LANES
+    block = lines * 8 // math.gcd(lines, 8)
+    values = recv_ref[...].astype(f32)
+    total = sum(values[k : k + block] for k in range(0, values.shape[0], block))
+    total = sum(total[k : k + lines] for k in range(0, block, lines))
+    rhs = jnp.concatenate(
+        [
+            jnp.concatenate([total[k : k + 1] for k in range(t, lines, own)], axis=1)
+            for t in range(own)
+        ],
+        axis=0,
+    )
     rhs_ref[...] = rhs
     low_ref[...] = rhs.astype(bf16)
-    coef_ref[...] = coefs_of(rhs, basis_ref)
+    send_coefs(group_ref, rhs, basis_ref, coef_ref)
 
 
 def near_kernel(pick_ref, blocks_ref, low_ref, other_ref, out_ref):
@@ -270,60 +329,63 @@
 
 
 def step_kernel(
-    index_ref, table_ref, couple_ref, target_ref, rhs_ref, near_ref, basis_ref, *out_refs
+    index_ref, group_ref, table_ref, couple_ref, target_ref, rhs_ref, near_ref, basis_ref, *out_refs
 ):
     clusters = rhs_ref.shape[0]
     far = jnp.concatenate(
         [far_of(index_ref, table_ref, couple_ref, target_ref, t) for t in range(clusters)], axis=0
     )
     density = rhs_ref[...] - near_ref[...] - far
-    out_refs[0][...] = density
-    if len(out_refs) > 1:
-        out_refs[1][...] = density.astype(bf16)
-        out_refs[2][...] = coefs_of(density, basis_ref)
-
-
-def start(received, basis):
+    if len(out_refs) == 1:
+        out_refs[0][...] = density
+    else:
+        out_refs[0][...] = density.astype(bf16)
+        send_coefs(group_ref, density, basis_ref, out_refs[1])
+
+
+def start(group, received, basis):
     clusters, rank, width = basis.shape
+    chips = lax.axis_size(CHIPS)
     return pl.pallas_call(
         start_kernel,
         out_shape=(
-            jax.ShapeDtypeStruct((clusters, width), f32),
-            jax.ShapeDtypeStruct((clusters, width), bf16),
-            jax.ShapeDtypeStruct((1, LANES), f32),
+            kept((clusters, width), f32),
+            kept((clusters, width), bf16),
+            kept((chips, LANES), f32),
         ),
-        in_specs=[VMEM] * 2,
+        in_specs=[SMEM] + [VMEM] * 2,
         out_specs=(VMEM,) * 3,
         cost_estimate=pl.CostEstimate(flops=500_000, bytes_accessed=400_000, transcendentals=0),
         name="start",
-    )(received, basis)
+    )(group, *held(received, basis))
 
 
 def near_part(pick, blocks, low, other):
     return pl.pallas_call(
         near_kernel,
-        out_shape=jax.ShapeDtypeStruct(low.shape, f32),
+        out_shape=kept(low.shape, f32),
         in_specs=[SMEM, VMEM, VMEM, VMEM],
         out_specs=VMEM,
         cost_estimate=pl.CostEstimate(flops=2_000_000, bytes_accessed=1_200_000, transcendentals=0),
         name="near_part",
-    )(pick, blocks, low, other)
-
-
-def step(index, table, couple, target, rhs, near, basis, last):
+    )(pick, *held(blocks, low, other))
+
+
+def step(index, group, table, couple, target, rhs, near, basis, last):
     clusters, rank, width = basis.shape
-    shapes = [jax.ShapeDtypeStruct((clusters, width), f32)]
-    if not last:
-        shapes.append(jax.ShapeDtypeStruct((clusters, width), bf16))
-        shapes.append(jax.ShapeDtypeStruct((1, LANES), f32))
+    chips = lax.axis_size(CHIPS)
+    if last:
+        shapes = [jax.ShapeDtypeStruct((clusters, width), f32)]
+    else:
+        shapes = [kept((clusters, width), bf16), kept((chips, LANES), f32)]
     return pl.pallas_call(
         step_kernel,
         out_shape=tuple(shapes),
-        in_specs=[SMEM] + [VMEM] * 6,
+        in_specs=[SMEM] * 2 + [VMEM] * 6,
         out_specs=(VMEM,) * len(shapes),
         cost_estimate=pl.CostEstimate(flops=500_000, bytes_accessed=500_000, transcendentals=0),
         name="step",
-    )(index, table, couple, target, rhs, near, basis)
+    )(index, group, *held(table, couple, target, rhs, near, basis))
 
 
 def local(
@@ -359,6 +421,14 @@
         "qs,asc->aqc", harmonic, shape_coef, preferred_element_type=jnp.float32
     ).astype(bf16)
 
+    basis = jnp.swapaxes(src_basis, 1, 2)
+
+    cores = lax.axis_size(CORE)
+    live = -(-quads // 16) * 16
+    sums = pair_sums(near_dest, near_slot, sources, centers, live, cores)
+    far_src, far_rank, sums = lax.optimization_barrier((far_src, far_rank, sums))
+    received = exchange_wall(sums, walls)
+
     source_rows = jnp.take(cluster_slot, far_src.reshape(-1), axis=0)
     per_row = LANES // rank
     index, offset = table_place(source_rows, clusters, rank)
@@ -370,59 +440,78 @@
     lane_part = jnp.arange(LANES, dtype=jnp.int32) // rank
     here = lane_part[None, None, None, :] == offset.reshape(far_src.shape)[:, :, None, None]
     couple = jnp.where(here, jnp.tile(masked, (1, 1, 1, per_row)), 0.0)
-    basis = jnp.swapaxes(src_basis, 1, 2)
-
-    target = near_slot * walls + near_dest
-    sums = pair_sums(target, sources, centers, walls)
-    received = exchange_wall(sums, clusters)
-    rhs, low, coef = start(received, basis)
+    chips = lax.axis_size(CHIPS)
+    groups = LANES // (clusters * rank)
+    group = (lax.axis_index(CHIPS) // (chips // groups)).astype(jnp.int32).reshape(1)
+    rhs, low, coef = start(group, received, basis)
     for k in range(ITERS):
         other = shifted(low, WALL, 1)
         near = near_part(near_pick, near_blocks, low, other)
         table = gather_all(coef, clusters, rank)
-        out = step(index, table, couple, tgt_basis, rhs, near, basis, k == ITERS - 1)
+        out = step(index, group, table, couple, tgt_basis, rhs, near, basis, k == ITERS - 1)
         if k < ITERS - 1:
-            density, low, coef = out
+            low, coef = out
         else:
             (density,) = out
     return (surface, density)
 
 
+def centers_kernel(spots_ref, out_ref):
+    own, width = spots_ref.shape
+    spots = spots_ref[...] * (FIXED / REACH)
+    lines = jnp.concatenate(
+        [spots[t : t + 1, k : k + LANES] for k in range(0, width, LANES) for t in range(own)],
+        axis=0,
+    )
+    lines = jnp.clip(jnp.round(lines), -FIXED, FIXED)
+    count = lines.shape[0]
+    copies = 16 // math.gcd(count, 16)
+    block = jnp.concatenate([lines] * copies, axis=0).astype(jnp.int32).astype(jnp.int16)
+    for k in range(0, out_ref.shape[0], count * copies):
+        out_ref[pl.ds(k, count * copies), :] = block
+
+
 def gather_wall(panel_centers):
-    walls = lax.axis_size(WALL)
-    flat = panel_centers.reshape(1, 1, -1)
-    pieces = jnp.broadcast_to(flat, (walls, 1, flat.shape[2]))
+    chips = lax.axis_size(CHIPS)
+    clusters, width = panel_centers.shape
+    pieces = pl.pallas_call(
+        centers_kernel,
+        out_shape=jax.ShapeDtypeStruct((chips * clusters * width // LANES, LANES), jnp.int16),
+        in_specs=[VMEM],
+        out_specs=VMEM,
+        cost_estimate=pl.CostEstimate(flops=10_000, bytes_accessed=50_000, transcendentals=0),
+        name="centers",
+    )(panel_centers)
+    pieces = pieces.reshape(-1, clusters, LANES)
+    pieces = lax.all_to_all(pieces, CHIPS, split_axis=0, concat_axis=0, tiled=True)
+    return lax.all_gather(pieces, CORE).reshape(-1, LANES)
+
+
+def exchange_wall(sums, walls):
+    pieces = sums.reshape(-1, OWN, LANES)
     pieces = lax.all_to_all(pieces, WALL, split_axis=0, concat_axis=0, tiled=True)
     return pieces.reshape(-1, LANES)
 
 
-def exchange_wall(sums, clusters):
-    walls = sums.shape[0]
-    pieces = sums.astype(bf16).reshape(walls, clusters, -1)
-    return lax.all_to_all(pieces, WALL, split_axis=0, concat_axis=0, tiled=True)
-
-
 def gather_all(coef, clusters, rank):
-    walls = lax.axis_size(WALL)
-    cells = lax.axis_size(CELLS)
+    chips = lax.axis_size(CHIPS)
+    peers = lax.axis_size(PLANE)
     groups = LANES // (clusters * rank)
-    lane = jnp.arange(LANES, dtype=jnp.int32) // (clusters * rank)
-    mine = jnp.where(lane[None, :] == lax.axis_index(WALL) // (walls // groups), coef, 0.0)
-    pieces = jnp.broadcast_to(mine[:, None, :], (walls, 1, LANES))
-    pieces = lax.all_to_all(pieces, WALL, split_axis=0, concat_axis=0, tiled=True)
-    group = jnp.sum(pieces.reshape(groups, walls // groups, LANES), axis=0)
-    pieces = jnp.broadcast_to(group.reshape(1, 1, -1), (cells, 1, group.size))
-    pieces = lax.all_to_all(pieces, CELLS, split_axis=0, concat_axis=0, tiled=True)
+    pieces = coef.reshape(chips, 1, LANES)
+    pieces = lax.all_to_all(pieces, CHIPS, split_axis=0, concat_axis=0, tiled=True)
+    own = jnp.sum(pieces.reshape(groups, chips // groups, LANES), axis=0)
+    pieces = jnp.broadcast_to(own.reshape(1, 1, -1), (peers, 1, own.size))
+    pieces = lax.all_to_all(pieces, PLANE, split_axis=0, concat_axis=0, tiled=True)
     return pieces.reshape(-1, LANES)
 
 
 def table_place(slots, clusters, rank):
-    walls = lax.axis_size(WALL)
+    chips, cores = lax.axis_size(CHIPS), lax.axis_size(CORE)
     groups = LANES // (clusters * rank)
-    lines = walls // groups
+    lines = chips // groups
     device = slots // clusters
-    cell, wall = device // walls, device % walls
-    return cell * lines + wall % lines, wall // lines * clusters + slots % clusters
+    cell, chip, core = device // (chips * cores), device // cores % chips, device % cores
+    return (cell * cores + core) * lines + chip % lines, chip // lines * clusters + slots % clusters
 
 
 def solution(mesh):

time: 221 us -> 192 us (0.87)
  Pallas kernels: 36.1 us -> 25.4 us
  local copies, waits for them, and re-layouts: 12.7 us -> 2.8 us
  waiting for transfers between devices: 101 us -> 94.8 us
  blocking collectives: 0 us -> 4.28 us
  other arithmetic: 4.96 us -> 0.9 us
    pallas_call x7 -> x8, Pallas kernels: 36.1 us -> 25.4 us  [the longest x1 15.1 us: pair_sums(): pl.pallas_call(functools.partial(pairs_kernel, cores), out_shape=jax.Shap...]
    all_to_all x6, waiting for transfers between devices: 101 us -> 94.8 us  [the longest x2 37.6 us: gather_all(): lax.all_to_all(pieces, CHIPS, split_axis=0, concat_axis=0, tiled=True)]
    all_gather x0 -> x1, blocking collectives: none -> 4.28 us  [gather_wall(): return lax.all_gather(pieces, CORE).reshape(-1, LANES)]
    unnamed x26 -> x22, local copies, waits for them, and re-layouts: 3.8 us -> 0.06 us
    all_to_all x6, starting transfers between devices: 59.4 us -> 55.8 us  [the longest x1 29.3 us: gather_wall(): lax.all_to_all(pieces, CHIPS, split_axis=0, concat_axis=0, tiled=True)]
    broadcast_in_dim x6 -> x2, local copies, waits for them, and re-layouts: 4.2 us -> 1.44 us  [gather_all(): pieces = jnp.broadcast_to(own.reshape(1, 1, -1), (peers, 1, own.size))]
    reshape x3 -> x0, local copies, waits for them, and re-layouts: 2.73 us -> none  [the longest x1 1.36 us: near_sources(): near_cell.reshape(rows, 1)]
  transfers between devices with their start and end apart: 8 -> 8, of which waited for: 6 -> 6; matrix products, arithmetic and copies ran while one was open for 4% -> 3% of each run, Pallas kernels for 4% -> 3%
where the time goes in v2:
time: 192 us; the launch traced here: 191 us
  waiting for transfers between devices  94.8 us (49%)
  starting transfers between devices  60.6 us (32%)
  Pallas kernels  25.4 us (13%)
  blocking collectives  4.28 us (2%)
  local copies, waits for them, and re-layouts  2.8 us (1%)
    all_to_all x2, waiting for transfers between devices, gather_all(): lax.all_to_all(pieces, CHIPS, split_axis=0, concat_axis=0, tiled=True)  37.6 us
    all_to_all x1, starting transfers between devices, gather_wall(): lax.all_to_all(pieces, CHIPS, split_axis=0, concat_axis=0, tiled=True)  29.3 us
    all_to_all x1, waiting for transfers between devices, exchange_wall(): lax.all_to_all(pieces, WALL, split_axis=0, concat_axis=0, tiled=True)  26.4 us
    all_to_all x1, waiting for transfers between devices, gather_wall(): lax.all_to_all(pieces, CHIPS, split_axis=0, concat_axis=0, tiled=True)  19.7 us
    pallas_call x1, Pallas kernels, pair_sums(): pl.pallas_call(functools.partial(pairs_kernel, cores), out_shape=jax.Shap...  15.1 us
    all_to_all x2, starting transfers between devices, gather_all(): lax.all_to_all(pieces, PLANE, split_axis=0, concat_axis=0, tiled=True)  14.5 us
    all_to_all x2, waiting for transfers between devices, gather_all(): lax.all_to_all(pieces, PLANE, split_axis=0, concat_axis=0, tiled=True)  11.1 us
    all_to_all x2, starting transfers between devices, gather_all(): lax.all_to_all(pieces, CHIPS, split_axis=0, concat_axis=0, tiled=True)  7.66 us
  transfers between devices with their start and end apart: 8, of which 6 were waited for; matrix products, arithmetic and copies ran while one was open for 3% of the time, Pallas kernels for 3%

profile of v2, /device:TPU:1, one launch (start us, length us, event | category | flops | bytes accessed | tf_op | source)
XLA Modules:
  0.0 191.3 jit_solution(3200602842341786075)
XLA Ops:
  0.7 1.3 centers.1
  2.0 29.3 %all-to-all-start = ((s16[96,2,128]{2,1,0:T(2,128)(2,1)}), s16[96,2,128]{2,1,0:T(2,128)(2,1)S(1)}, u32[]{:S(2)}, u32[]{:S(2)}) async-start(s16[96,2,128]{2,1,0:T(2,128)(2,1)} %bitcast.43), calls=%async_computation | async-start | bytes 98304 | tf_op jit(solution)/shard_map/all_to_all | solution.py:486
  31.3 2.9 %near_sources.1.src_ref = bf16[6,64,640]{2,1,0:T(8,128)(2,1)S(1)} custom-call(s32[1,64]{1,0:T(1,128)} %bitcast.49, bf16[3,289,256]{2,1,0:T(8,128)(2,1)} %shape_ref.1, bf16[3,289,256]{2,1,0:T(8,128)(2,1)} %force_ref.1, bf16[289,640]{1,0:T(8,128)(2,1)} %constant.152.grid_ref), custom_call_target="tpu_custom_call" | custom-call | flops 200000000 | bytes 2500000 | tf_op jit(solution)/shard_map/near_sources/pallas_call | solution.py:111
  34.2 19.7 %all-to-all-done = s16[96,2,128]{2,1,0:T(2,128)(2,1)S(1)} async-done(((s16[96,2,128]{2,1,0:T(2,128)(2,1)}), s16[96,2,128]{2,1,0:T(2,128)(2,1)S(1)}, u32[]{:S(2)}, u32[]{:S(2)}) %all-to-all-start) | async-done | bytes 49184 | tf_op jit(solution)/shard_map/all_to_all | solution.py:486
  54.0 4.3 %all-gather = s16[192,2,128]{2,1,0:T(2,128)(2,1)S(1)} all-gather(s16[96,2,128]{2,1,0:T(2,128)(2,1)S(1)} %all-to-all-done), channel_id=2, replica_groups=mesh['cells_0'=4,'cells_1'=4,'wall_0'=32,'wall_1'=2] {'wall_1'}, dimensions={0}, use_global_device_ids=true | all-gather | bytes 147456 | tf_op jit(solution)/shard_map/all_gather | solution.py:487
  58.3 15.1 %pair_sums.1 = bf16[384,128]{1,0:T(8,128)(2,1)} custom-call(s32[1,64]{1,0:T(1,128)S(1)} %bitcast.41, s32[1,64]{1,0:T(1,128)S(1)} %bitcast.42, bf16[6,64,640]{2,1,0:T(8,128)(2,1)S(1)} %near_sources.1.src_ref, s16[384,128]{1,0:T(8,128)(2,1)S(1)} %bitcast.40), custom_call_target="tpu_custom_call" | custom-call | flops 1000000000 | bytes 1000000 | tf_op jit(solution)/shard_map/pair_sums/pallas_call | solution.py:244
  73.6 4.4 %all-to-all-start.1 = ((bf16[192,2,128]{2,1,0:T(2,128)(2,1)}), bf16[192,2,128]{2,1,0:T(2,128)(2,1)S(1)}, u32[]{:S(2)}, u32[]{:S(2)}) async-start(bf16[192,2,128]{2,1,0:T(2,128)(2,1)} %bitcast.44), calls=%async_computation.1 | async-start | bytes 196608 | tf_op jit(solution)/shard_map/all_to_all | solution.py:492
  78.1 0.7 gather_fusion
  78.7 0.1 gather.7
  78.8 0.1 and_select_fusion
  78.9 0.1 tile.4
  79.1 0.3 tile.10
  79.5 26.4 %all-to-all-done.1 = bf16[192,2,128]{2,1,0:T(2,128)(2,1)S(1)} async-done(((bf16[192,2,128]{2,1,0:T(2,128)(2,1)}), bf16[192,2,128]{2,1,0:T(2,128)(2,1)S(1)}, u32[]{:S(2)}, u32[]{:S(2)}) %all-to-all-start.1) | async-done | bytes 98336 | tf_op jit(solution)/shard_map/all_to_all | solution.py:492
  105.9 0.9 start.1
  106.8 3.8 %all-to-all-start.2 = ((f32[32,1,128]{2,1,0:T(1,128)}), f32[32,1,128]{2,1,0:T(1,128)S(1)}, u32[]{:S(2)}, u32[]{:S(2)}) async-start(f32[32,1,128]{2,1,0:T(1,128)} %bitcast.13), calls=%async_computation.2 | async-start | bytes 32768 | tf_op jit(solution)/shard_map/all_to_all | solution.py:501
  110.7 3.1 %collective-permute-start = (bf16[2,384]{1,0:T(2,128)(2,1)S(1)}, bf16[2,384]{1,0:T(2,128)(2,1)S(1)}, u32[]{:S(2)}, u32[]{:S(2)}) collective-permute-start(bf16[2,384]{1,0:T(2,128)(2,1)S(1)} %get-tuple-element.15.low_ref), channel_id=1, source_target_pairs={{0,1},{1,2},{2,3},{3,4},{4,5},{5,6},{6,7},{7,8},{8,9},{9,10},{10,1... | collective-permute-start | bytes 4616 | tf_op jit(solution)/shard_map/ppermute | solution.py:36
  113.8 18.1 %all-to-all-done.2 = f32[32,1,128]{2,1,0:T(1,128)S(1)} async-done(((f32[32,1,128]{2,1,0:T(1,128)}), f32[32,1,128]{2,1,0:T(1,128)S(1)}, u32[]{:S(2)}, u32[]{:S(2)}) %all-to-all-start.2) | async-done | bytes 16416 | tf_op jit(solution)/shard_map/all_to_all | solution.py:501
  131.9 0.7 broadcast_in_dim.37
  132.6 9.4 %all-to-all-start.3 = ((f32[32,1,1024]{2,1,0:T(1,128)}), f32[32,1,1024]{2,1,0:T(1,128)S(1)}, u32[]{:S(2)}, u32[]{:S(2)}) async-start(f32[32,1,1024]{2,1,0:T(1,128)} %broadcast_in_dim.37), calls=%async_computation.3 | async-start | bytes 262144 | tf_op jit(solution)/shard_map/all_to_all | solution.py:504
  142.1 0.6 fusion.4.index_ref
  142.6 1.1 near_part.2.near_ref
  143.7 6.0 %all-to-all-done.3 = f32[32,1,1024]{2,1,0:T(1,128)S(1)} async-done(((f32[32,1,1024]{2,1,0:T(1,128)}), f32[32,1,1024]{2,1,0:T(1,128)S(1)}, u32[]{:S(2)}, u32[]{:S(2)}) %all-to-all-start.3) | async-done | bytes 131104 | tf_op jit(solution)/shard_map/all_to_all | solution.py:504
  149.7 1.6 step.2
  151.4 3.8 %all-to-all-start.4 = ((f32[32,1,128]{2,1,0:T(1,128)}), f32[32,1,128]{2,1,0:T(1,128)S(1)}, u32[]{:S(2)}, u32[]{:S(2)}) async-start(f32[32,1,128]{2,1,0:T(1,128)} %bitcast.18), calls=%async_computation.4 | async-start | bytes 32768 | tf_op jit(solution)/shard_map/all_to_all | solution.py:501
  155.2 1.7 collective-permute-start.1
  156.9 19.5 %all-to-all-done.4 = f32[32,1,128]{2,1,0:T(1,128)S(1)} async-done(((f32[32,1,128]{2,1,0:T(1,128)}), f32[32,1,128]{2,1,0:T(1,128)S(1)}, u32[]{:S(2)}, u32[]{:S(2)}) %all-to-all-start.4) | async-done | bytes 16416 | tf_op jit(solution)/shard_map/all_to_all | solution.py:501
  176.4 0.7 broadcast_in_dim.42
  177.1 5.1 %all-to-all-start.5 = ((f32[32,1,1024]{2,1,0:T(1,128)}), f32[32,1,1024]{2,1,0:T(1,128)S(1)}, u32[]{:S(2)}, u32[]{:S(2)}) async-start(f32[32,1,1024]{2,1,0:T(1,128)} %broadcast_in_dim.42), calls=%async_computation.5 | async-start | bytes 262144 | tf_op jit(solution)/shard_map/all_to_all | solution.py:504
  182.2 1.6 fusion
  183.8 1.1 near_part.3.near_ref
  184.9 5.1 %all-to-all-done.5 = f32[32,1,1024]{2,1,0:T(1,128)S(1)} async-done(((f32[32,1,1024]{2,1,0:T(1,128)}), f32[32,1,1024]{2,1,0:T(1,128)S(1)}, u32[]{:S(2)}, u32[]{:S(2)}) %all-to-all-start.5) | async-done | bytes 131104 | tf_op jit(solution)/shard_map/all_to_all | solution.py:504
  190.0 1.4 step.3
  (35 shorter events, 0.5 us)
Async XLA Ops:
  0.6 77.4 %copy-start = (s32[2048]{0:T(1024)S(1)}, s32[2048]{0:T(1024)}, u32[]{:S(2)}) copy-start(s32[2048]{0:T(1024)} %param.29) | copy-start | bytes 24580
  0.6 57.6 %copy-start.4 = (s32[64]{0:T(128)S(1)}, s32[64]{0:T(128)}, u32[]{:S(2)}) copy-start(s32[64]{0:T(128)} %param.19) | copy-start | bytes 772
  0.7 57.6 %copy-start.5 = (s32[64]{0:T(128)S(1)}, s32[64]{0:T(128)}, u32[]{:S(2)}) copy-start(s32[64]{0:T(128)} %param.20) | copy-start | bytes 772
  2.0 52.0 %all-to-all-start = ((s16[96,2,128]{2,1,0:T(2,128)(2,1)}), s16[96,2,128]{2,1,0:T(2,128)(2,1)S(1)}, u32[]{:S(2)}, u32[]{:S(2)}) async-start(s16[96,2,128]{2,1,0:T(2,128)(2,1)} %bitcast.43), calls=%async_computation | async-start | bytes 98304 | tf_op jit(solution)/shard_map/all_to_all | solution.py:486
  58.3 15.1 %copy-start.9 = (s32[2,8]{1,0:T(2,128)S(1)}, s32[2,8]{1,0:T(2,128)}, u32[]{:S(2)}) copy-start(s32[2,8]{1,0:T(2,128)} %param.26) | copy-start | bytes 196
  58.3 19.7 %copy-start.8 = (s32[2,8]{1,0:T(2,128)S(1)}, s32[2,8]{1,0:T(2,128)}, u32[]{:S(2)}) copy-start(s32[2,8]{1,0:T(2,128)} %param.27) | copy-start | bytes 196
  58.3 20.6 %copy-start.7 = (f32[2,8,16,16]{3,2,1,0:T(8,128)S(1)}, f32[2,8,16,16]{3,2,1,0:T(8,128)}, u32[]{:S(2)}) copy-start(f32[2,8,16,16]{3,2,1,0:T(8,128)} %param.25) | copy-start | bytes 49156
  73.6 32.4 %all-to-all-start.1 = ((bf16[192,2,128]{2,1,0:T(2,128)(2,1)}), bf16[192,2,128]{2,1,0:T(2,128)(2,1)S(1)}, u32[]{:S(2)}, u32[]{:S(2)}) async-start(bf16[192,2,128]{2,1,0:T(2,128)(2,1)} %bitcast.44), calls=%async_computation.1 | async-start | bytes 196608 | tf_op jit(solution)/shard_map/all_to_all | solution.py:492
  78.9 27.0 %copy-start.2 = (f32[2,384,16]{1,2,0:T(8,128)S(1)}, f32[2,384,16]{1,2,0:T(8,128)}, u32[]{:S(2)}) copy-start(f32[2,384,16]{1,2,0:T(8,128)} %param.24) | copy-start | bytes 147460
  79.1 63.6 %copy-start.1 = (bf16[2,2,384,384]{3,2,1,0:T(8,128)(2,1)S(1)}, bf16[2,2,384,384]{3,2,1,0:T(8,128)(2,1)}, u32[]{:S(2)}) copy-start(bf16[2,2,384,384]{3,2,1,0:T(8,128)(2,1)} %blocks_ref.3) | copy-start | bytes 3538948
  79.4 70.4 %copy-start.3 = (f32[2,16,384]{2,1,0:T(8,128)S(1)}, f32[2,16,384]{2,1,0:T(8,128)}, u32[]{:S(2)}) copy-start(f32[2,16,384]{2,1,0:T(8,128)} %target_ref.3) | copy-start | bytes 147460
  106.8 25.1 %all-to-all-start.2 = ((f32[32,1,128]{2,1,0:T(1,128)}), f32[32,1,128]{2,1,0:T(1,128)S(1)}, u32[]{:S(2)}, u32[]{:S(2)}) async-start(f32[32,1,128]{2,1,0:T(1,128)} %bitcast.13), calls=%async_computation.2 | async-start | bytes 32768 | tf_op jit(solution)/shard_map/all_to_all | solution.py:501
  110.7 32.0 %collective-permute-start = (bf16[2,384]{1,0:T(2,128)(2,1)S(1)}, bf16[2,384]{1,0:T(2,128)(2,1)S(1)}, u32[]{:S(2)}, u32[]{:S(2)}) collective-permute-start(bf16[2,384]{1,0:T(2,128)(2,1)S(1)} %get-tuple-element.15.low_ref), channel_id=1, source_target_pairs={{0,1},{1,2},{2,3},{3,4},{4,5},{5,6},{6,7},{7,8},{8,9},{9,10},{10,1... | collective-permute-start | bytes 4616 | tf_op jit(solution)/shard_map/ppermute | solution.py:36
  131.9 50.3 %copy-start.6 = (bf16[3,289,256]{2,1,0:T(8,128)(2,1)S(1)}, bf16[3,289,256]{2,1,0:T(8,128)(2,1)}, u32[]{:S(2)}) copy-start(bf16[3,289,256]{2,1,0:T(8,128)(2,1)} %shape_ref.1) | copy-start | bytes 1331716
  131.9 50.3 %copy-start.10 = (bf16[578,289,1]{0,1,2:T(8,128)(2,1)S(1)}, bf16[578,289,1]{0,1,2:T(8,128)(2,1)}, u32[]{:S(2)}) copy-start(bf16[578,289,1]{0,1,2:T(8,128)(2,1)} %constant.153) | copy-start | bytes 1002256
  132.6 17.1 %all-to-all-start.3 = ((f32[32,1,1024]{2,1,0:T(1,128)}), f32[32,1,1024]{2,1,0:T(1,128)S(1)}, u32[]{:S(2)}, u32[]{:S(2)}) async-start(f32[32,1,1024]{2,1,0:T(1,128)} %broadcast_in_dim.37), calls=%async_computation.3 | async-start | bytes 262144 | tf_op jit(solution)/shard_map/all_to_all | solution.py:504
  151.4 25.0 %all-to-all-start.4 = ((f32[32,1,128]{2,1,0:T(1,128)}), f32[32,1,128]{2,1,0:T(1,128)S(1)}, u32[]{:S(2)}, u32[]{:S(2)}) async-start(f32[32,1,128]{2,1,0:T(1,128)} %bitcast.18), calls=%async_computation.4 | async-start | bytes 32768 | tf_op jit(solution)/shard_map/all_to_all | solution.py:501
  155.2 28.6 %collective-permute-start.1 = (bf16[2,384]{1,0:T(2,128)(2,1)S(1)}, bf16[2,384]{1,0:T(2,128)(2,1)S(1)}, u32[]{:S(2)}, u32[]{:S(2)}) collective-permute-start(bf16[2,384]{1,0:T(2,128)(2,1)S(1)} %get-tuple-element.17.low_ref), channel_id=1, source_target_pairs={{0,1},{1,2},{2,3},{3,4},{4,5},{5,6},{6,7},{7,8},{8,9},{9,10},{10,1... | collective-permute-start | bytes 4616 | tf_op jit(solution)/shard_map/ppermute | solution.py:36
  177.1 12.9 %all-to-all-start.5 = ((f32[32,1,1024]{2,1,0:T(1,128)}), f32[32,1,1024]{2,1,0:T(1,128)S(1)}, u32[]{:S(2)}, u32[]{:S(2)}) async-start(f32[32,1,1024]{2,1,0:T(1,128)} %broadcast_in_dim.42), calls=%async_computation.5 | async-start | bytes 262144 | tf_op jit(solution)/shard_map/all_to_all | solution.py:504

commit v3 on v2

--- a/solution.py
+++ b/solution.py
@@ -136,8 +136,8 @@
     rows, quads = src_ref.shape[1], src_ref.shape[2]
     lines = OWN * 3
     walls = out_ref.shape[0] // lines
-    third = len(bufs) // 3
-    rho_bufs, inv_bufs, cube_bufs = bufs[:third], bufs[third : 2 * third], bufs[2 * third :]
+    half = len(bufs) // 2
+    rho_bufs, pow_bufs = bufs[:half], bufs[half:]
     pan = PANELS
     own = OWN
     clusters = walls * own
@@ -188,22 +188,21 @@
     lanes = len(rho_bufs) // 2
 
     def turn(i, old, new):
-        held_inv, held_cube = inv_bufs[old::2], cube_bufs[old::2]
-        next_inv, next_cube = inv_bufs[new::2], cube_bufs[new::2]
+        held_pow, next_pow = pow_bufs[old::2], pow_bufs[new::2]
         held_rho, next_rho = rho_bufs[old::2], rho_bufs[new::2]
         for n in range(lanes):
             r = jnp.clip(lanes * (i - 2) + n, n, rows - lanes + n)
             g = get(gsc, r, rows)
             g_hi = g.astype(bf16)
             g_lo = (g - g_hi.astype(f32)).astype(bf16)
-            first = dot_nt(jnp.concatenate([g_hi, g_lo], axis=0), held_cube[n][...])
-            plain = dot_nt(g_hi, held_inv[n][...])
-            mom[pl.ds(r, 16, stride=rows), :] = first[:16] + first[16:]
-            mom[pl.ds(16 * rows + r, 8, stride=rows), :] = plain[:8]
+            both = jnp.concatenate([g_hi, g_lo], axis=0)
+            sums = jnp.transpose(dot_nt(held_pow[n][...], both))
+            mom[pl.ds(r, 16, stride=rows), :] = sums[:16, :pan] + sums[16:, :pan]
+            mom[pl.ds(16 * rows + r, 8, stride=rows), :] = sums[:8, pan:]
         for n in range(lanes):
             inverse = lax.rsqrt(held_rho[n][...])
-            next_inv[n][...] = inverse.astype(bf16)
-            next_cube[n][...] = (inverse * inverse * inverse).astype(bf16)
+            next_pow[n][pl.ds(0, pan), :] = (inverse * inverse * inverse).astype(bf16)
+            next_pow[n][pl.ds(pan, pan), :] = inverse.astype(bf16)
         for n in range(lanes):
             r = jnp.minimum(lanes * i + n, rows - lanes + n)
             yr = get(ysc, r, rows).astype(bf16)
@@ -234,11 +233,11 @@
     out_ref[...] = csc[...].astype(out_ref.dtype)
 
 
-PAIR_LANES = 4
-TURN_UNROLL = 1
-
-
-def pair_sums(dest, slot, sources, centers, live, cores):
+PAIR_LANES = 2
+TURN_UNROLL = 4
+
+
+def pair_sums(dest, slot, sources, centers, cores):
     rows, quads = sources.shape[1:]
     pan = PANELS
     return pl.pallas_call(
@@ -255,7 +254,7 @@
             pltpu.VMEM(centers.shape, f32),
         ]
         + [pltpu.VMEM((pan, quads), f32)] * (2 * PAIR_LANES)
-        + [pltpu.VMEM((pan, quads), bf16)] * (4 * PAIR_LANES),
+        + [pltpu.VMEM((2 * pan, quads), bf16)] * (2 * PAIR_LANES),
         cost_estimate=pl.CostEstimate(
             flops=1_000_000_000, bytes_accessed=1_000_000, transcendentals=5_000_000
         ),
@@ -424,8 +423,7 @@
     basis = jnp.swapaxes(src_basis, 1, 2)
 
     cores = lax.axis_size(CORE)
-    live = -(-quads // 16) * 16
-    sums = pair_sums(near_dest, near_slot, sources, centers, live, cores)
+    sums = pair_sums(near_dest, near_slot, sources, centers, cores)
     far_src, far_rank, sums = lax.optimization_barrier((far_src, far_rank, sums))
     received = exchange_wall(sums, walls)
 

time: 192 us -> 190 us (0.990)
  no operation moved by 1% of the time
where the time goes in v3:
time: 190 us
  waiting for transfers between devices  94.8 us (50%)
  starting transfers between devices  60.7 us (32%)
  Pallas kernels  23.8 us (13%)
  blocking collectives  4.28 us (2%)
  local copies, waits for them, and re-layouts  2.8 us (1%)
    all_to_all x2, waiting for transfers between devices, gather_all(): lax.all_to_all(pieces, CHIPS, split_axis=0, concat_axis=0, tiled=True)  37.6 us
    all_to_all x1, starting transfers between devices, gather_wall(): lax.all_to_all(pieces, CHIPS, split_axis=0, concat_axis=0, tiled=True)  29.3 us
    all_to_all x1, waiting for transfers between devices, exchange_wall(): lax.all_to_all(pieces, WALL, split_axis=0, concat_axis=0, tiled=True)  26.4 us
    all_to_all x1, waiting for transfers between devices, gather_wall(): lax.all_to_all(pieces, CHIPS, split_axis=0, concat_axis=0, tiled=True)  19.7 us
    all_to_all x2, starting transfers between devices, gather_all(): lax.all_to_all(pieces, PLANE, split_axis=0, concat_axis=0, tiled=True)  14.5 us
    pallas_call x1, Pallas kernels, pair_sums(): pl.pallas_call(functools.partial(pairs_kernel, cores), out_shape=jax.Shap...  13.5 us
    all_to_all x2, waiting for transfers between devices, gather_all(): lax.all_to_all(pieces, PLANE, split_axis=0, concat_axis=0, tiled=True)  11.1 us
    all_to_all x2, starting transfers between devices, gather_all(): lax.all_to_all(pieces, CHIPS, split_axis=0, concat_axis=0, tiled=True)  7.66 us
  transfers between devices with their start and end apart: 8, of which 6 were waited for; matrix products, arithmetic and copies ran while one was open for 3% of the time, Pallas kernels for 3%

profile of v3, /device:TPU:1, one launch (start us, length us, event | category | flops | bytes accessed | tf_op | source)
XLA Modules:
  0.0 189.7 jit_solution(11283577736132511586)
XLA Ops:
  0.7 1.3 centers.1
  2.0 29.3 %all-to-all-start = ((s16[96,2,128]{2,1,0:T(2,128)(2,1)}), s16[96,2,128]{2,1,0:T(2,128)(2,1)S(1)}, u32[]{:S(2)}, u32[]{:S(2)}) async-start(s16[96,2,128]{2,1,0:T(2,128)(2,1)} %bitcast.43), calls=%async_computation | async-start | bytes 98304 | tf_op jit(solution)/shard_map/all_to_all | solution.py:484
  31.3 2.9 %near_sources.1.src_ref = bf16[6,64,640]{2,1,0:T(8,128)(2,1)S(1)} custom-call(s32[1,64]{1,0:T(1,128)} %bitcast.49, bf16[3,289,256]{2,1,0:T(8,128)(2,1)} %shape_ref.1, bf16[3,289,256]{2,1,0:T(8,128)(2,1)} %force_ref.1, bf16[289,640]{1,0:T(8,128)(2,1)} %constant.152.grid_ref), custom_call_target="tpu_custom_call" | custom-call | flops 200000000 | bytes 2500000 | tf_op jit(solution)/shard_map/near_sources/pallas_call | solution.py:111
  34.2 19.7 %all-to-all-done = s16[96,2,128]{2,1,0:T(2,128)(2,1)S(1)} async-done(((s16[96,2,128]{2,1,0:T(2,128)(2,1)}), s16[96,2,128]{2,1,0:T(2,128)(2,1)S(1)}, u32[]{:S(2)}, u32[]{:S(2)}) %all-to-all-start) | async-done | bytes 49184 | tf_op jit(solution)/shard_map/all_to_all | solution.py:484
  54.0 4.3 %all-gather = s16[192,2,128]{2,1,0:T(2,128)(2,1)S(1)} all-gather(s16[96,2,128]{2,1,0:T(2,128)(2,1)S(1)} %all-to-all-done), channel_id=2, replica_groups=mesh['cells_0'=4,'cells_1'=4,'wall_0'=32,'wall_1'=2] {'wall_1'}, dimensions={0}, use_global_device_ids=true | all-gather | bytes 147456 | tf_op jit(solution)/shard_map/all_gather | solution.py:485
  58.3 13.5 %pair_sums.1 = bf16[384,128]{1,0:T(8,128)(2,1)} custom-call(s32[1,64]{1,0:T(1,128)S(1)} %bitcast.41, s32[1,64]{1,0:T(1,128)S(1)} %bitcast.42, bf16[6,64,640]{2,1,0:T(8,128)(2,1)S(1)} %near_sources.1.src_ref, s16[384,128]{1,0:T(8,128)(2,1)S(1)} %bitcast.40), custom_call_target="tpu_custom_call" | custom-call | flops 1000000000 | bytes 1000000 | tf_op jit(solution)/shard_map/pair_sums/pallas_call | solution.py:243
  71.9 4.4 %all-to-all-start.1 = ((bf16[192,2,128]{2,1,0:T(2,128)(2,1)}), bf16[192,2,128]{2,1,0:T(2,128)(2,1)S(1)}, u32[]{:S(2)}, u32[]{:S(2)}) async-start(bf16[192,2,128]{2,1,0:T(2,128)(2,1)} %bitcast.44), calls=%async_computation.1 | async-start | bytes 196608 | tf_op jit(solution)/shard_map/all_to_all | solution.py:490
  76.5 0.7 gather_fusion
  77.1 0.1 gather.7
  77.2 0.1 and_select_fusion
  77.3 0.1 tile.4
  77.4 0.3 tile.10
  77.9 26.4 %all-to-all-done.1 = bf16[192,2,128]{2,1,0:T(2,128)(2,1)S(1)} async-done(((bf16[192,2,128]{2,1,0:T(2,128)(2,1)}), bf16[192,2,128]{2,1,0:T(2,128)(2,1)S(1)}, u32[]{:S(2)}, u32[]{:S(2)}) %all-to-all-start.1) | async-done | bytes 98336 | tf_op jit(solution)/shard_map/all_to_all | solution.py:490
  104.3 0.9 start.1
  105.2 3.8 %all-to-all-start.2 = ((f32[32,1,128]{2,1,0:T(1,128)}), f32[32,1,128]{2,1,0:T(1,128)S(1)}, u32[]{:S(2)}, u32[]{:S(2)}) async-start(f32[32,1,128]{2,1,0:T(1,128)} %bitcast.13), calls=%async_computation.2 | async-start | bytes 32768 | tf_op jit(solution)/shard_map/all_to_all | solution.py:499
  109.0 3.1 %collective-permute-start = (bf16[2,384]{1,0:T(2,128)(2,1)S(1)}, bf16[2,384]{1,0:T(2,128)(2,1)S(1)}, u32[]{:S(2)}, u32[]{:S(2)}) collective-permute-start(bf16[2,384]{1,0:T(2,128)(2,1)S(1)} %get-tuple-element.15.low_ref), channel_id=1, source_target_pairs={{0,1},{1,2},{2,3},{3,4},{4,5},{5,6},{6,7},{7,8},{8,9},{9,10},{10,1... | collective-permute-start | bytes 4616 | tf_op jit(solution)/shard_map/ppermute | solution.py:36
  112.2 18.1 %all-to-all-done.2 = f32[32,1,128]{2,1,0:T(1,128)S(1)} async-done(((f32[32,1,128]{2,1,0:T(1,128)}), f32[32,1,128]{2,1,0:T(1,128)S(1)}, u32[]{:S(2)}, u32[]{:S(2)}) %all-to-all-start.2) | async-done | bytes 16416 | tf_op jit(solution)/shard_map/all_to_all | solution.py:499
  130.3 0.7 broadcast_in_dim.37
  131.0 9.5 %all-to-all-start.3 = ((f32[32,1,1024]{2,1,0:T(1,128)}), f32[32,1,1024]{2,1,0:T(1,128)S(1)}, u32[]{:S(2)}, u32[]{:S(2)}) async-start(f32[32,1,1024]{2,1,0:T(1,128)} %broadcast_in_dim.37), calls=%async_computation.3 | async-start | bytes 262144 | tf_op jit(solution)/shard_map/all_to_all | solution.py:502
  140.5 0.6 fusion.4.index_ref
  141.0 1.1 near_part.2.near_ref
  142.1 6.0 %all-to-all-done.3 = f32[32,1,1024]{2,1,0:T(1,128)S(1)} async-done(((f32[32,1,1024]{2,1,0:T(1,128)}), f32[32,1,1024]{2,1,0:T(1,128)S(1)}, u32[]{:S(2)}, u32[]{:S(2)}) %all-to-all-start.3) | async-done | bytes 131104 | tf_op jit(solution)/shard_map/all_to_all | solution.py:502
  148.1 1.6 step.2
  149.8 3.8 %all-to-all-start.4 = ((f32[32,1,128]{2,1,0:T(1,128)}), f32[32,1,128]{2,1,0:T(1,128)S(1)}, u32[]{:S(2)}, u32[]{:S(2)}) async-start(f32[32,1,128]{2,1,0:T(1,128)} %bitcast.18), calls=%async_computation.4 | async-start | bytes 32768 | tf_op jit(solution)/shard_map/all_to_all | solution.py:499
  153.6 1.7 collective-permute-start.1
  155.3 19.5 %all-to-all-done.4 = f32[32,1,128]{2,1,0:T(1,128)S(1)} async-done(((f32[32,1,128]{2,1,0:T(1,128)}), f32[32,1,128]{2,1,0:T(1,128)S(1)}, u32[]{:S(2)}, u32[]{:S(2)}) %all-to-all-start.4) | async-done | bytes 16416 | tf_op jit(solution)/shard_map/all_to_all | solution.py:499
  174.8 0.7 broadcast_in_dim.42
  175.5 5.1 %all-to-all-start.5 = ((f32[32,1,1024]{2,1,0:T(1,128)}), f32[32,1,1024]{2,1,0:T(1,128)S(1)}, u32[]{:S(2)}, u32[]{:S(2)}) async-start(f32[32,1,1024]{2,1,0:T(1,128)} %broadcast_in_dim.42), calls=%async_computation.5 | async-start | bytes 262144 | tf_op jit(solution)/shard_map/all_to_all | solution.py:502
  180.6 1.6 fusion
  182.2 1.1 near_part.3.near_ref
  183.3 5.1 %all-to-all-done.5 = f32[32,1,1024]{2,1,0:T(1,128)S(1)} async-done(((f32[32,1,1024]{2,1,0:T(1,128)}), f32[32,1,1024]{2,1,0:T(1,128)S(1)}, u32[]{:S(2)}, u32[]{:S(2)}) %all-to-all-start.5) | async-done | bytes 131104 | tf_op jit(solution)/shard_map/all_to_all | solution.py:502
  188.3 1.3 step.3
  (35 shorter events, 0.5 us)
Async XLA Ops:
  0.6 75.8 %copy-start = (s32[2048]{0:T(1024)S(1)}, s32[2048]{0:T(1024)}, u32[]{:S(2)}) copy-start(s32[2048]{0:T(1024)} %param.29) | copy-start | bytes 24580
  0.6 57.6 %copy-start.4 = (s32[64]{0:T(128)S(1)}, s32[64]{0:T(128)}, u32[]{:S(2)}) copy-start(s32[64]{0:T(128)} %param.19) | copy-start | bytes 772
  0.7 57.6 %copy-start.5 = (s32[64]{0:T(128)S(1)}, s32[64]{0:T(128)}, u32[]{:S(2)}) copy-start(s32[64]{0:T(128)} %param.20) | copy-start | bytes 772
  2.0 52.0 %all-to-all-start = ((s16[96,2,128]{2,1,0:T(2,128)(2,1)}), s16[96,2,128]{2,1,0:T(2,128)(2,1)S(1)}, u32[]{:S(2)}, u32[]{:S(2)}) async-start(s16[96,2,128]{2,1,0:T(2,128)(2,1)} %bitcast.43), calls=%async_computation | async-start | bytes 98304 | tf_op jit(solution)/shard_map/all_to_all | solution.py:484
  58.3 13.5 %copy-start.9 = (s32[2,8]{1,0:T(2,128)S(1)}, s32[2,8]{1,0:T(2,128)}, u32[]{:S(2)}) copy-start(s32[2,8]{1,0:T(2,128)} %param.26) | copy-start | bytes 196
  58.3 18.1 %copy-start.8 = (s32[2,8]{1,0:T(2,128)S(1)}, s32[2,8]{1,0:T(2,128)}, u32[]{:S(2)}) copy-start(s32[2,8]{1,0:T(2,128)} %param.27) | copy-start | bytes 196
  58.3 18.9 %copy-start.7 = (f32[2,8,16,16]{3,2,1,0:T(8,128)S(1)}, f32[2,8,16,16]{3,2,1,0:T(8,128)}, u32[]{:S(2)}) copy-start(f32[2,8,16,16]{3,2,1,0:T(8,128)} %param.25) | copy-start | bytes 49156
  71.9 32.4 %all-to-all-start.1 = ((bf16[192,2,128]{2,1,0:T(2,128)(2,1)}), bf16[192,2,128]{2,1,0:T(2,128)(2,1)S(1)}, u32[]{:S(2)}, u32[]{:S(2)}) async-start(bf16[192,2,128]{2,1,0:T(2,128)(2,1)} %bitcast.44), calls=%async_computation.1 | async-start | bytes 196608 | tf_op jit(solution)/shard_map/all_to_all | solution.py:490
  77.3 27.0 %copy-start.2 = (f32[2,384,16]{1,2,0:T(8,128)S(1)}, f32[2,384,16]{1,2,0:T(8,128)}, u32[]{:S(2)}) copy-start(f32[2,384,16]{1,2,0:T(8,128)} %param.24) | copy-start | bytes 147460
  77.4 63.6 %copy-start.1 = (bf16[2,2,384,384]{3,2,1,0:T(8,128)(2,1)S(1)}, bf16[2,2,384,384]{3,2,1,0:T(8,128)(2,1)}, u32[]{:S(2)}) copy-start(bf16[2,2,384,384]{3,2,1,0:T(8,128)(2,1)} %blocks_ref.3) | copy-start | bytes 3538948
  77.8 70.4 %copy-start.3 = (f32[2,16,384]{2,1,0:T(8,128)S(1)}, f32[2,16,384]{2,1,0:T(8,128)}, u32[]{:S(2)}) copy-start(f32[2,16,384]{2,1,0:T(8,128)} %target_ref.3) | copy-start | bytes 147460
  105.2 25.1 %all-to-all-start.2 = ((f32[32,1,128]{2,1,0:T(1,128)}), f32[32,1,128]{2,1,0:T(1,128)S(1)}, u32[]{:S(2)}, u32[]{:S(2)}) async-start(f32[32,1,128]{2,1,0:T(1,128)} %bitcast.13), calls=%async_computation.2 | async-start | bytes 32768 | tf_op jit(solution)/shard_map/all_to_all | solution.py:499
  109.0 32.0 %collective-permute-start = (bf16[2,384]{1,0:T(2,128)(2,1)S(1)}, bf16[2,384]{1,0:T(2,128)(2,1)S(1)}, u32[]{:S(2)}, u32[]{:S(2)}) collective-permute-start(bf16[2,384]{1,0:T(2,128)(2,1)S(1)} %get-tuple-element.15.low_ref), channel_id=1, source_target_pairs={{0,1},{1,2},{2,3},{3,4},{4,5},{5,6},{6,7},{7,8},{8,9},{9,10},{10,1... | collective-permute-start | bytes 4616 | tf_op jit(solution)/shard_map/ppermute | solution.py:36
  130.3 50.3 %copy-start.6 = (bf16[3,289,256]{2,1,0:T(8,128)(2,1)S(1)}, bf16[3,289,256]{2,1,0:T(8,128)(2,1)}, u32[]{:S(2)}) copy-start(bf16[3,289,256]{2,1,0:T(8,128)(2,1)} %shape_ref.1) | copy-start | bytes 1331716
  130.3 50.3 %copy-start.10 = (bf16[578,289,1]{0,1,2:T(8,128)(2,1)S(1)}, bf16[578,289,1]{0,1,2:T(8,128)(2,1)}, u32[]{:S(2)}) copy-start(bf16[578,289,1]{0,1,2:T(8,128)(2,1)} %constant.153) | copy-start | bytes 1002256
  131.0 17.1 %all-to-all-start.3 = ((f32[32,1,1024]{2,1,0:T(1,128)}), f32[32,1,1024]{2,1,0:T(1,128)S(1)}, u32[]{:S(2)}, u32[]{:S(2)}) async-start(f32[32,1,1024]{2,1,0:T(1,128)} %broadcast_in_dim.37), calls=%async_computation.3 | async-start | bytes 262144 | tf_op jit(solution)/shard_map/all_to_all | solution.py:502
  149.8 25.0 %all-to-all-start.4 = ((f32[32,1,128]{2,1,0:T(1,128)}), f32[32,1,128]{2,1,0:T(1,128)S(1)}, u32[]{:S(2)}, u32[]{:S(2)}) async-start(f32[32,1,128]{2,1,0:T(1,128)} %bitcast.18), calls=%async_computation.4 | async-start | bytes 32768 | tf_op jit(solution)/shard_map/all_to_all | solution.py:499
  153.6 28.6 %collective-permute-start.1 = (bf16[2,384]{1,0:T(2,128)(2,1)S(1)}, bf16[2,384]{1,0:T(2,128)(2,1)S(1)}, u32[]{:S(2)}, u32[]{:S(2)}) collective-permute-start(bf16[2,384]{1,0:T(2,128)(2,1)S(1)} %get-tuple-element.17.low_ref), channel_id=1, source_target_pairs={{0,1},{1,2},{2,3},{3,4},{4,5},{5,6},{6,7},{7,8},{8,9},{9,10},{10,1... | collective-permute-start | bytes 4616 | tf_op jit(solution)/shard_map/ppermute | solution.py:36
  175.5 12.9 %all-to-all-start.5 = ((f32[32,1,1024]{2,1,0:T(1,128)}), f32[32,1,1024]{2,1,0:T(1,128)S(1)}, u32[]{:S(2)}, u32[]{:S(2)}) async-start(f32[32,1,1024]{2,1,0:T(1,128)} %broadcast_in_dim.42), calls=%async_computation.5 | async-start | bytes 262144 | tf_op jit(solution)/shard_map/all_to_all | solution.py:502
